TPU v7x, 512 devices: a whole 4x4x16 slice. The times are simulated.
512 devices in a mesh: depth: 4 (over z_hi, core), plane: 128 (over x, z_lo, y).
Axes of the slice: x: 4, y: 4, z: 16 (z_hi: 2, z_lo: 8; z = z_hi * 8 + z_lo), core: 2. Of those that a mesh axis runs over, the one named last changes fastest.
Arguments:
- magnet: float32 [3, 32, 512, 1024], P(None, 'depth', 'plane'), may hold values from -1 to 1, as said below
- mask: int32 [512, 1024], P('plane'), may hold values 0 or 1
- materials: int32 [32], P('depth'), may hold values from 0 to 3
- exchange_strength: float32 [4], replicated, may hold values from 0.5 to 2
- anisotropy: float32 [4], replicated, may hold values from 0.5 to 3
- damping: float32 [4], replicated, may hold values from 0.05 to 0.6
- source_strength: float32 [4], replicated, may hold values from 0.3 to 1.5
- thermal_strength: float32 [4], replicated, may hold values from 0.5 to 2
- pivots: float32 [32, 3, 3], replicated, may hold values from -1 to 1, as said below
- lower: float32 [32, 3, 3], replicated, may hold values from -1 to 1, as said below
- upper: float32 [32, 3, 3], replicated, may hold values from -1 to 1, as said below
- noise_stream: int32 [1], replicated, may hold values from 0 to 999999
- counter: int32 [1], replicated, may hold values from 0 to 99999
Outputs:
- magnet_next: float32 [3, 32, 512, 1024], P(None, 'depth', 'plane')
- accumulation: float32 [3, 32, 512, 1024], P(None, 'depth', 'plane')
Inputs may be any that keep to these rules, and one draw needn't show every extreme that they name: `magnet`: unit vectors. `pivots`: each block has spectral norm below 0.98. `lower`: each block has spectral norm below 1. `upper`: each block has spectral norm below 1.
All inputs are finite; a program needn't handle non-finite values. No bound on the sum of `mask` on one device may be relied on, other than what follows from the above.
Results may differ from a plain program's by a relative error of at most 0.000073.
Values sent between devices are 32-bit elements; how exact they have to be, the bound alone decides.
A program may use at most 128 MiB of HBM per device.

v0:
```python
import jax
import jax.numpy as jnp
from jax import lax
from jax.sharding import PartitionSpec as P


def padded(block, sides, width, periodic):
    for axis, dim in sides:
        count = lax.axis_size(axis)
        forward = [(i, i + 1) for i in range(count - 1)]
        if periodic:
            forward.append((count - 1, 0))
        backward = [(target, source) for source, target in forward]
        low = lax.ppermute(
            lax.slice_in_dim(block, block.shape[dim] - width, None, axis=dim), axis, forward
        )
        high = lax.ppermute(lax.slice_in_dim(block, 0, width, axis=dim), axis, backward)
        block = jnp.concatenate([low, block, high], axis=dim)
    return block


def cross(a, b):
    return jnp.stack(
        [a[1] * b[2] - a[2] * b[1], a[2] * b[0] - a[0] * b[2], a[0] * b[1] - a[1] * b[0]]
    )


def apply_block(block, vec):
    return jnp.stack(
        [
            block[row, 0] * vec[0] + block[row, 1] * vec[1] + block[row, 2] * vec[2]
            for row in range(3)
        ]
    )


def forward_sweep(source, pivots, lower, initial):
    previous = initial
    values = []
    for layer_pos in range(source.shape[1]):
        previous = apply_block(
            pivots[layer_pos], source[:, layer_pos] - apply_block(lower[layer_pos], previous)
        )
        values.append(previous)
    return values


def backward_sweep(values, upper, initial):
    after = initial
    solved = [None] * len(values)
    for layer_pos in range(len(values) - 1, -1, -1):
        after = values[layer_pos] - apply_block(upper[layer_pos], after)
        solved[layer_pos] = after
    return solved


def solve_columns(source, pivots, lower, upper):
    zero_state = jnp.zeros_like(source[:, 0])
    values = forward_sweep(source, pivots, lower, zero_state)
    return jnp.stack(backward_sweep(values, upper, zero_state), axis=1)


def hash_uniform(index, stream, counter):
    mixed = index * 739982445 + stream * 695872825 + counter * 1597334677
    mixed = mixed ^ lax.shift_right_logical(mixed, jnp.int32(16))
    mixed = mixed * 739982445
    mixed = mixed ^ lax.shift_right_logical(mixed, jnp.int32(15))
    mixed = mixed * 695872825
    mixed = mixed ^ lax.shift_right_logical(mixed, jnp.int32(16))
    return (mixed & 65535).astype(jnp.float32) / 32767.5 - 1.0


def layer_values(materials, table):
    onehot = (materials[:, None] == jnp.arange(table.shape[0], dtype=jnp.int32)[None, :]).astype(
        jnp.float32
    )
    return jnp.sum(onehot * table[None, :], axis=1)[None, :, None, None]


def normalize(vec):
    return vec / jnp.sqrt(jnp.sum(vec * vec, axis=0, keepdims=True))


def spin_solve(source, pivots, lower, upper):
    columns = lax.all_to_all(source, "depth", split_axis=3, concat_axis=1, tiled=True)
    solved = solve_columns(columns, pivots, lower, upper)
    return lax.all_to_all(solved, "depth", split_axis=1, concat_axis=3, tiled=True)


def local(
    magnet,
    mask,
    materials,
    exchange_strength,
    anisotropy,
    damping,
    source_strength,
    thermal_strength,
    pivots,
    lower,
    upper,
    noise_stream,
    counter,
):
    depth_local = magnet.shape[1]
    row_local = magnet.shape[2]
    width_y = magnet.shape[3]
    total_layers = depth_local * lax.axis_size("depth")
    total_rows = row_local * lax.axis_size("plane")
    maskf = mask.astype(jnp.float32)[None, None]
    stiff = layer_values(materials, exchange_strength)
    aniso = layer_values(materials, anisotropy)
    alpha = layer_values(materials, damping)
    beta = layer_values(materials, source_strength)
    theta = layer_values(materials, thermal_strength)
    comp = jnp.arange(3, dtype=jnp.int32)[:, None, None, None]
    layer = (lax.axis_index("depth") * depth_local + jnp.arange(depth_local, dtype=jnp.int32))[
        None, :, None, None
    ]
    xrow = (lax.axis_index("plane") * row_local + jnp.arange(row_local, dtype=jnp.int32))[
        None, None, :, None
    ]
    ycol = jnp.arange(width_y, dtype=jnp.int32)[None, None, None, :]
    index = ((comp * total_layers + layer) * total_rows + xrow) * width_y + ycol
    noise = theta * hash_uniform(index, noise_stream[0], counter[0])
    axis_z = jnp.array([0.0, 0.0, 1.0], dtype=jnp.float32)[:, None, None, None]

    def rate(field):
        masked = field * maskf
        wide = padded(masked, (("plane", 2),), 2, True)
        near = (
            wide[:, :, 3 : row_local + 3]
            + wide[:, :, 1 : row_local + 1]
            + jnp.roll(masked, 1, 3)
            + jnp.roll(masked, -1, 3)
        )
        far = (
            wide[:, :, 4 : row_local + 4]
            + wide[:, :, 0:row_local]
            + jnp.roll(masked, 2, 3)
            + jnp.roll(masked, -2, 3)
        )
        planar = 4.0 / 3.0 * near - 1.0 / 12.0 * far
        stacked = padded(masked, (("depth", 1),), 1, False)
        vertical = stacked[:, 2:] + stacked[:, :-2]
        accum = spin_solve(beta * field, pivots, lower, upper)
        heff = stiff * (planar + 0.5 * vertical) + aniso * field * axis_z + noise + 0.5 * accum
        torque = cross(field, heff)
        change = -(torque + alpha * cross(field, torque)) / (1.0 + alpha * alpha) * maskf
        return (change, accum)

    first, _ = rate(magnet)
    middle = normalize(magnet + 0.03 * first)
    second, accum = rate(middle)
    magnet_next = normalize(magnet + 0.015 * (first + second))
    return (magnet_next, accum)


def solution(mesh):
    placed = (
        P(None, "depth", "plane", None),
        P("plane", None),
        P("depth"),
        P(),
        P(),
        P(),
        P(),
        P(),
        P(),
        P(),
        P(),
        P(),
        P(),
    )
    return jax.shard_map(
        local,
        mesh=mesh,
        in_specs=placed,
        out_specs=(P(None, "depth", "plane", None), P(None, "depth", "plane", None)),
        check_vma=False,
    )
```

profile of v0, /device:TPU:1, one launch (start us, length us, event | category | flops | bytes accessed | tf_op | source)
XLA Modules:
  0.0 1309.7 jit_solution(13437907100284906902)
XLA Ops:
  8.7 9.2 reshape.5395
  17.9 16.6 %all-to-all-start = ((f32[4,1,24576]{2,1,0:T(1,128)}), f32[4,1,24576]{2,1,0:T(1,128)S(1)}, u32[]{:S(2)}, u32[]{:S(2)}) async-start(f32[4,1,24576]{2,1,0:T(1,128)} %reshape.5395), calls=%async_computation | async-start | bytes 786432 | tf_op jit(solution)/shard_map/all_to_all | solution.py:85
  35.2 10.0 collective-permute-start
  50.1 12.4 collective-permute-start.3
  116.1 10.3 reshape.5396
  132.2 7.5 multiply_add_fusion.555
  143.6 7.5 multiply_add_fusion.549
  154.7 7.4 multiply_add_fusion.543
  166.0 7.5 multiply_add_fusion.537
  177.2 7.6 multiply_add_fusion.531
  188.8 7.6 multiply_add_fusion.525
  200.2 7.8 multiply_add_fusion.519
  211.7 7.5 multiply_add_fusion.513
  223.0 7.6 multiply_add_fusion.507
  234.3 7.6 multiply_add_fusion.501
  257.0 7.6 multiply_add_fusion.489
  268.4 7.6 multiply_add_fusion.483
  279.6 7.5 multiply_add_fusion.477
  290.9 7.6 multiply_add_fusion.471
  302.1 7.4 multiply_add_fusion.465
  313.2 7.4 multiply_add_fusion.459
  324.5 7.5 multiply_add_fusion.453
  335.8 7.6 multiply_add_fusion.447
  358.2 7.5 multiply_add_fusion.435
  369.5 7.6 multiply_add_fusion.429
  403.2 7.5 multiply_add_fusion.411
  414.6 7.6 multiply_add_fusion.405
  426.0 7.5 multiply_add_fusion.399
  448.3 7.5 multiply_add_fusion.387
  459.7 7.5 multiply_add_fusion.381
  471.1 7.5 multiply_add_fusion.375
  667.1 17.5 %all-to-all-done.1 = f32[3,32,4,256]{3,2,0,1:T(4,128)S(1)} async-done(((f32[3,32,4,256]{3,2,0,1:T(4,128)}), f32[3,32,4,256]{3,2,0,1:T(4,128)S(1)}, u32[]{:S(2)}, u32[]{:S(2)}) %all-to-all-start.1) | async-done | bytes 393248 | tf_op jit(solution)/shard_map/all_to_all | solution.py:87
  692.0 9.2 reshape.5397
  701.2 10.9 all-to-all-start.2
  712.9 13.0 collective-permute-start.4
  729.8 10.3 reshape.5398
  745.5 7.5 multiply_add_fusion.276
  756.9 7.5 multiply_add_fusion.270
  768.1 7.4 multiply_add_fusion.264
  779.3 7.5 multiply_add_fusion.258
  790.5 7.6 multiply_add_fusion.252
  802.1 7.6 multiply_add_fusion.246
  813.6 7.8 multiply_add_fusion.240
  825.0 7.5 multiply_add_fusion.234
  836.3 7.6 multiply_add_fusion.228
  847.7 7.6 multiply_add_fusion.222
  870.3 7.6 multiply_add_fusion.210
  881.7 7.6 multiply_add_fusion.204
  892.9 7.5 multiply_add_fusion.198
  904.2 7.6 multiply_add_fusion.192
  926.5 7.4 multiply_add_fusion.180
  937.8 7.5 multiply_add_fusion.174
  949.1 7.6 multiply_add_fusion.168
  971.5 7.5 multiply_add_fusion.156
  982.8 7.6 multiply_add_fusion.150
  994.1 7.4 multiply_add_fusion.144
  1016.4 7.5 multiply_add_fusion.132
  1027.8 7.6 multiply_add_fusion.126
  1039.2 7.5 multiply_add_fusion.120
  1061.6 7.5 multiply_add_fusion.108
  1072.9 7.5 multiply_add_fusion.102
  1084.4 7.5 multiply_add_fusion.96
  1275.8 12.3 all-to-all-start.3
  1290.7 12.4 collective-permute-start.7
  (484 shorter events, 757.2 us)
Async XLA Ops:
  2.7 1.3 copy-start.6
  2.8 663.3 %copy-start.10 = (f32[8]{0:T(128)}, f32[8]{0:T(128)S(1)}, u32[]{:S(2)}) copy-start(f32[8]{0:T(128)S(1)} %get-tuple-element.104) | copy-start | bytes 100
  4.0 58.5 %copy-start.1 = (f32[32,3,3]{0,2,1:T(4,128)S(1)}, f32[32,3,3]{0,2,1:T(4,128)}, u32[]{:S(2)}) copy-start(f32[32,3,3]{0,2,1:T(4,128)} %param.23) | copy-start | bytes 3460
  4.0 59.0 %copy-start.2 = (f32[32,3,3]{0,2,1:T(4,128)S(1)}, f32[32,3,3]{0,2,1:T(4,128)}, u32[]{:S(2)}) copy-start(f32[32,3,3]{0,2,1:T(4,128)} %param.22) | copy-start | bytes 3460
  4.0 59.5 %copy-start.3 = (f32[32,3,3]{0,2,1:T(4,128)S(1)}, f32[32,3,3]{0,2,1:T(4,128)}, u32[]{:S(2)}) copy-start(f32[32,3,3]{0,2,1:T(4,128)} %param.24) | copy-start | bytes 3460
  17.9 95.9 %all-to-all-start = ((f32[4,1,24576]{2,1,0:T(1,128)}), f32[4,1,24576]{2,1,0:T(1,128)S(1)}, u32[]{:S(2)}, u32[]{:S(2)}) async-start(f32[4,1,24576]{2,1,0:T(1,128)} %reshape.5395), calls=%async_computation | async-start | bytes 786432 | tf_op jit(solution)/shard_map/all_to_all | solution.py:85
  35.2 649.5 %collective-permute-start = (f32[3,8,2,1024]{3,1,2,0:T(8,128)}, f32[3,8,2,1024]{3,1,2,0:T(8,128)S(1)}, u32[]{:S(2)}, u32[]{:S(2)}) collective-permute-start(f32[3,8,2,1024]{3,1,2,0:T(8,128)} %get-tuple-element.427), channel_id=1, source_target_pairs={{1,0},{2,1},{3,2},{4,3},{5,4},{6,5},{7,6},{8,7},{9,8},{10,9},{11,1... | collective-permute-start | bytes 589832 | tf_op jit(solution)/shard_map/ppermute | solution.py:17
  45.3 639.5 %collective-permute-start.1 = (f32[3,8,2,1024]{3,1,2,0:T(8,128)}, f32[3,8,2,1024]{3,1,2,0:T(8,128)}, u32[]{:S(2)}, u32[]{:S(2)}) collective-permute-start(f32[3,8,2,1024]{3,1,2,0:T(8,128)} %get-tuple-element.428), channel_id=1, source_target_pairs={{0,1},{1,2},{2,3},{3,4},{4,5},{5,6},{6,7},{7,8},{8,9},{9,10},{10,1... | collective-permute-start | bytes 589832 | tf_op jit(solution)/shard_map/ppermute | solution.py:14
  47.9 636.8 %collective-permute-start.2 = (f32[3,1,4,1024]{3,1,2,0:T(1,128)}, f32[3,1,4,1024]{3,1,2,0:T(1,128)}, u32[]{:S(2)}, u32[]{:S(2)}) collective-permute-start(f32[3,1,4,1024]{3,1,2,0:T(1,128)} %get-tuple-element.425), channel_id=1, source_target_pairs={{128,0},{256,128},{384,256},{129,1},{257,129},{385,257},{130,2},{2... | collective-permute-start | bytes 147464 | tf_op jit(solution)/shard_map/ppermute | solution.py:17
  50.1 634.6 %collective-permute-start.3 = (f32[3,1,4,1024]{3,1,2,0:T(1,128)}, f32[3,1,4,1024]{3,1,2,0:T(1,128)}, u32[]{:S(2)}, u32[]{:S(2)}) collective-permute-start(f32[3,1,4,1024]{3,1,2,0:T(1,128)} %get-tuple-element.426), channel_id=1, source_target_pairs={{0,128},{128,256},{256,384},{1,129},{129,257},{257,385},{2,130},{1... | collective-permute-start | bytes 147464 | tf_op jit(solution)/shard_map/ppermute | solution.py:14
  107.4 24.7 %copy-start.8 = (f32[3]{0:T(128)}, f32[3]{0:T(128)S(1)}, u32[]{:S(2)}) copy-start(f32[3]{0:T(128)S(1)} %maximum_maximum_fusion.1) | copy-start | bytes 40
  107.5 554.2 %copy-start.4 = (f32[3]{0:T(128)}, f32[3]{0:T(128)S(1)}, u32[]{:S(2)}) copy-start(f32[3]{0:T(128)S(1)} %maximum_maximum_fusion) | copy-start | bytes 40
  369.4 315.3 %copy-start = (f32[3,8,4,1024]{3,2,1,0:T(4,128)S(1)}, f32[3,8,4,1024]{3,2,1,0:T(4,128)}, u32[]{:S(2)}) copy-start(f32[3,8,4,1024]{3,2,1,0:T(4,128)} %param.14) | copy-start | bytes 1179652
  662.6 22.0 %all-to-all-start.1 = ((f32[3,32,4,256]{3,2,0,1:T(4,128)}), f32[3,32,4,256]{3,2,0,1:T(4,128)S(1)}, u32[]{:S(2)}, u32[]{:S(2)}) async-start(f32[3,32,4,256]{3,2,0,1:T(4,128)} %copy.279), calls=%async_computation.1 | async-start | bytes 786432 | tf_op jit(solution)/shard_map/all_to_all | solution.py:87
  684.6 2.1 copy-start.11
  684.6 2.1 copy-start.13
  684.6 2.5 copy-start.7
  701.2 26.8 %all-to-all-start.2 = ((f32[4,1,24576]{2,1,0:T(1,128)}), f32[4,1,24576]{2,1,0:T(1,128)S(1)}, u32[]{:S(2)}, u32[]{:S(2)}) async-start(f32[4,1,24576]{2,1,0:T(1,128)} %reshape.5397), calls=%async_computation.2 | async-start | bytes 786432 | tf_op jit(solution)/shard_map/all_to_all | solution.py:85
  712.9 593.0 %collective-permute-start.4 = (f32[3,8,2,1024]{3,1,2,0:T(8,128)}, f32[3,8,2,1024]{3,1,2,0:T(8,128)}, u32[]{:S(2)}, u32[]{:S(2)}) collective-permute-start(f32[3,8,2,1024]{3,1,2,0:T(8,128)} %get-tuple-element.415), channel_id=1, source_target_pairs={{1,0},{2,1},{3,2},{4,3},{5,4},{6,5},{7,6},{8,7},{9,8},{10,9},{11,1... | collective-permute-start | bytes 589832 | tf_op jit(solution)/shard_map/ppermute | solution.py:17
  726.0 580.0 %collective-permute-start.5 = (f32[3,8,2,1024]{3,1,2,0:T(8,128)}, f32[3,8,2,1024]{3,1,2,0:T(8,128)}, u32[]{:S(2)}, u32[]{:S(2)}) collective-permute-start(f32[3,8,2,1024]{3,1,2,0:T(8,128)} %get-tuple-element.416), channel_id=1, source_target_pairs={{0,1},{1,2},{2,3},{3,4},{4,5},{5,6},{6,7},{7,8},{8,9},{9,10},{10,1... | collective-permute-start | bytes 589832 | tf_op jit(solution)/shard_map/ppermute | solution.py:14
  729.8 15.6 %copy-start.9 = (f32[3]{0:T(128)S(1)}, f32[3]{0:T(128)}, u32[]{:S(2)}) copy-start(f32[3]{0:T(128)} %copy-done.8) | copy-start | bytes 40
  740.1 360.8 %copy-start.5 = (f32[3]{0:T(128)S(1)}, f32[3]{0:T(128)}, u32[]{:S(2)}) copy-start(f32[3]{0:T(128)} %copy-done.4) | copy-start | bytes 40
  1275.8 29.0 %all-to-all-start.3 = ((f32[3,32,4,256]{3,2,0,1:T(4,128)}), f32[3,32,4,256]{3,2,0,1:T(4,128)S(1)}, u32[]{:S(2)}, u32[]{:S(2)}) async-start(f32[3,32,4,256]{3,2,0,1:T(4,128)} %copy.319), calls=%async_computation.3 | async-start | bytes 786432 | tf_op jit(solution)/shard_map/all_to_all | solution.py:87
  1288.8 17.1 %collective-permute-start.6 = (f32[3,1,4,1024]{3,1,2,0:T(1,128)}, f32[3,1,4,1024]{3,1,2,0:T(1,128)}, u32[]{:S(2)}, u32[]{:S(2)}) collective-permute-start(f32[3,1,4,1024]{3,1,2,0:T(1,128)} %get-tuple-element.413), channel_id=1, source_target_pairs={{128,0},{256,128},{384,256},{129,1},{257,129},{385,257},{130,2},{2... | collective-permute-start | bytes 147464 | tf_op jit(solution)/shard_map/ppermute | solution.py:17
  1290.7 15.2 %collective-permute-start.7 = (f32[3,1,4,1024]{3,1,2,0:T(1,128)}, f32[3,1,4,1024]{3,1,2,0:T(1,128)}, u32[]{:S(2)}, u32[]{:S(2)}) collective-permute-start(f32[3,1,4,1024]{3,1,2,0:T(1,128)} %get-tuple-element.414), channel_id=1, source_target_pairs={{0,128},{128,256},{256,384},{1,129},{129,257},{257,385},{2,130},{1... | collective-permute-start | bytes 147464 | tf_op jit(solution)/shard_map/ppermute | solution.py:14
  1304.9 3.2 copy-start.12
  1304.9 3.2 copy-start.14
where the time goes:
time: 1330 us; the launch traced here: 1310 us
  other arithmetic  1070 us (80%)
  local copies, waits for them, and re-layouts  106 us (8%)
  starting transfers between devices  99.2 us (7%)
  waiting for transfers between devices  17.6 us (1%)
  between operations  16.5 us (1%)
    add x186, other arithmetic, apply_block(): block[row, 0] * vec[0] + block[row, 1] * vec[1] + block[row, 2] * vec[2]  1040 us
    unnamed x36, local copies, waits for them, and re-layouts  41 us
    slice x49, local copies, waits for them, and re-layouts, apply_block(): block[row, 0] * vec[0] + block[row, 1] * vec[1] + block[row, 2] * vec[2]  34.9 us
    ppermute x4, starting transfers between devices, padded(): lax.ppermute(lax.slice_in_dim(block, block.shape[dim] - width, None, axis...  28.8 us
    all_to_all x2, starting transfers between devices, spin_solve(): lax.all_to_all(source, 'depth', split_axis=3, concat_axis=1, tiled=True)  27.5 us
    ppermute x4, starting transfers between devices, padded(): lax.ppermute(lax.slice_in_dim(block, 0, width, axis=dim), axis, backward)  27.1 us
  transfers between devices with their start and end apart: 12, of which 1 were waited for; matrix products, arithmetic and copies ran while one was open for 87% of the time, Pallas kernels for 0%

commit v1 on v0

v1 whole, which is shorter than its diff:
```python
import functools

import jax
import jax.numpy as jnp
from jax import lax
from jax.experimental import pallas as pl
from jax.experimental.pallas import tpu as pltpu
from jax.sharding import PartitionSpec as P

MESH = pl.DeviceIdType.MESH
LANES = 128
SUB = 8
K1 = 739982445
K2 = 695872825
K3 = 1597334677


def wrap32(value):
    value &= 0xFFFFFFFF
    return value - (1 << 32) if value >= (1 << 31) else value


def cross(a, b):
    return [a[1] * b[2] - a[2] * b[1], a[2] * b[0] - a[0] * b[2], a[0] * b[1] - a[1] * b[0]]


def apply(block, vec):
    return [block[r][0] * vec[0] + block[r][1] * vec[1] + block[r][2] * vec[2] for r in range(3)]


def sub3(a, b):
    return [a[c] - b[c] for c in range(3)]


def add3(a, b):
    return [a[c] + b[c] for c in range(3)]


def shift_right(value, amount):
    return lax.shift_right_logical(value, jnp.full(value.shape, amount, jnp.int32))


def kernel(
    layers,
    rows,
    magnet_ref,
    mask_ref,
    mat_ref,
    stiff_ref,
    aniso_ref,
    damp_ref,
    source_ref,
    theta_ref,
    piv_ref,
    low_ref,
    up_ref,
    stream_ref,
    count_ref,
    next_ref,
    accum_ref,
    base,
    field,
    masked,
    noise,
    rest,
    sweep,
    maskf,
    coef,
    unit_y,
    halo_lo,
    halo_hi,
    edge_lo,
    edge_hi,
    state_out,
    state_in,
    send_sem,
    recv_sem,
):
    depth_id = lax.axis_index("depth")
    plane_id = lax.axis_index("plane")
    depth_count = lax.axis_size("depth")
    plane_count = lax.axis_size("plane")
    total_layers = layers * depth_count
    total_rows = rows * plane_count
    left = lax.rem(plane_id + plane_count - 1, plane_count)
    right = lax.rem(plane_id + 1, plane_count)
    above = depth_id + 1
    below = depth_id - 1
    has_below = depth_id > 0
    has_above = depth_id < depth_count - 1
    first_layer = depth_id * layers

    barrier = pltpu.get_barrier_semaphore()
    pl.semaphore_signal(barrier, inc=1, device_id=(depth_id, left), device_id_type=MESH)
    pl.semaphore_signal(barrier, inc=1, device_id=(depth_id, right), device_id_type=MESH)

    @pl.when(has_below)
    def _():
        pl.semaphore_signal(barrier, inc=1, device_id=(below, plane_id), device_id_type=MESH)

    @pl.when(has_above)
    def _():
        pl.semaphore_signal(barrier, inc=1, device_id=(above, plane_id), device_id_type=MESH)

    lane = lax.broadcasted_iota(jnp.int32, (SUB, LANES), 1)
    sublane = lax.broadcasted_iota(jnp.int32, (SUB, LANES), 0)

    def block_of(ref, layer):
        return [[ref[i, j, layer] for j in range(3)] for i in range(3)]

    for x in range(rows):
        maskf[x] = mask_ref[pl.ds(x, SUB, stride=rows), :].astype(jnp.float32)

    def load_layer(l, carry):
        for c in range(3):
            for x in range(rows):
                value = magnet_ref[c, l, pl.ds(x, SUB, stride=rows), :]
                base[x, l, c] = value
                field[x, l, c] = value
                masked[x, 1 + l, c] = value * maskf[x]
        return carry

    lax.fori_loop(0, layers, load_layer, 0)

    def unit(offset, c):
        return (lane == offset + c).astype(jnp.float32)

    zeros = jnp.zeros((SUB, LANES), jnp.float32)

    def unit_sweep(start, count, inject, finish):
        def down(i, y):
            y = [
                jnp.where(lane // 16 == 1, jnp.where(i == inject, unit(16, c), y[c]), y[c])
                for c in range(3)
            ]
            y = apply(block_of(piv_ref, start + i), apply(block_of(low_ref, start + i), y))
            y = [-y[c] for c in range(3)]
            for c in range(3):
                unit_y[i, c] = y[c]
            return tuple(y)

        last = lax.fori_loop(0, count, down, tuple(unit(0, c) for c in range(3)))

        def up(k, s):
            i = count - 1 - k
            s = apply(block_of(up_ref, start + i), s)
            return tuple(unit_y[i, c] - s[c] for c in range(3))

        mid = lax.fori_loop(0, count - finish, up, tuple(unit(32, c) for c in range(3)))
        first = lax.fori_loop(count - finish, count, up, mid)
        return last, mid, first

    def splat(slot, vec, offset):
        for r in range(3):
            for j in range(3):
                coef[slot, r * 3 + j] = jnp.broadcast_to(
                    vec[r][:, offset + j : offset + j + 1], (SUB, LANES)
                )

    last, _, first = unit_sweep(first_layer, layers, 0, 0)
    splat(0, last, 0)
    splat(1, first, 0)
    splat(2, first, 32)
    half = 2 * layers
    _, mid, first = unit_sweep(half, 2 * layers, layers, layers)
    splat(3, first, 0)
    splat(4, mid, 16)

    def matrix(slot):
        return [[coef[slot, r * 3 + j] for j in range(3)] for r in range(3)]

    pl.semaphore_wait(
        barrier, 2 + has_below.astype(jnp.int32) + has_above.astype(jnp.int32)
    )

    def remote(slot, src, dst, device):
        return pltpu.make_async_remote_copy(
            src_ref=src,
            dst_ref=dst,
            send_sem=send_sem.at[slot],
            recv_sem=recv_sem.at[slot],
            device_id=device,
            device_id_type=MESH,
        )

    def coefficient(ref, l):
        return ref[mat_ref[l]]

    for stage in range(2):
        slot = 8 * stage
        to_left = remote(
            slot, masked.at[0:2, 1 : layers + 1], halo_hi.at[stage], (depth_id, left)
        )
        to_right = remote(
            slot + 1, masked.at[rows - 2 : rows, 1 : layers + 1], halo_lo.at[stage], (depth_id, right)
        )
        edge_up = remote(slot + 2, masked.at[:, layers], edge_lo.at[stage], (above, plane_id))
        edge_down = remote(slot + 3, masked.at[:, 1], edge_hi.at[stage], (below, plane_id))
        to_left.start()
        to_right.start()

        @pl.when(has_above)
        def _():
            edge_up.start()

        @pl.when(has_below)
        def _():
            edge_down.start()

        def sources(l):
            beta = coefficient(source_ref, l)
            return [beta * field[:, l, c] for c in range(3)]

        def down(l, y):
            t = sub3(sources(l), apply(block_of(low_ref, first_layer + l), y))
            y = apply(block_of(piv_ref, first_layer + l), t)
            for c in range(3):
                sweep[:, l, c] = y[c]
            return tuple(y)

        def up(k, s):
            l = layers - 1 - k
            s = apply(block_of(up_ref, first_layer + l), s)
            return tuple(sweep[:, l, c] - s[c] for c in range(3))

        nothing = tuple(jnp.zeros((rows, SUB, LANES), jnp.float32) for _ in range(3))
        end = lax.fori_loop(0, layers, down, nothing)
        begin = lax.fori_loop(0, layers, up, nothing)

        for c in range(3):
            state_out[0, :, c] = end[c]
            state_out[1, :, c] = begin[c]
            state_out[3, :, c] = nothing[c]
            state_out[4, :, c] = nothing[c]

        def read(ref, index):
            return [ref[index, :, c] for c in range(3)]

        def write(index, value):
            for c in range(3):
                state_out[index, :, c] = value[c]

        is0, is1, is2, is3 = (depth_id == k for k in range(4))
        send_first_up = remote(slot + 4, state_out.at[0], state_in.at[stage, 0], (above, plane_id))
        send_first_down = remote(slot + 4, state_out.at[1], state_in.at[stage, 0], (below, plane_id))
        across_up = remote(slot + 5, state_out.at[2], state_in.at[stage, 1], (above, plane_id))
        across_down = remote(slot + 5, state_out.at[2], state_in.at[stage, 1], (below, plane_id))
        back_down = remote(slot + 6, state_out.at[5], state_in.at[stage, 2], (below, plane_id))
        back_up = remote(slot + 6, state_out.at[5], state_in.at[stage, 2], (above, plane_id))

        @pl.when(is0)
        def _():
            send_first_up.start()

        @pl.when(is3)
        def _():
            send_first_down.start()

        @pl.when(is1)
        def _():
            send_first_up.wait_recv()
            outer = read(state_in.at[stage], 0)
            write(3, outer)
            write(2, add3(read(state_out, 0), apply(matrix(0), outer)))
            across_up.start()

        @pl.when(is2)
        def _():
            send_first_down.wait_recv()
            outer = read(state_in.at[stage], 0)
            inner = add3(outer, apply(matrix(4), read(state_out, 0)))
            write(2, add3(read(state_out, 1), apply(matrix(2), inner)))
            across_down.start()

        if stage == 0:
            flat = (sublane * LANES + lane) * K1
            offset = stream_ref[0] * wrap32(K2) + count_ref[0] * wrap32(K3)

            def noise_layer(l, carry):
                theta = coefficient(theta_ref, l)
                for c in range(3):
                    for x in range(rows):
                        q = c * total_layers + first_layer + l
                        q = q * total_rows + plane_id * rows + x
                        h = flat + ((q * (SUB * LANES)) * K1 + offset)
                        h = h ^ shift_right(h, 16)
                        h = h * K1
                        h = h ^ shift_right(h, 15)
                        h = h * K2
                        h = h ^ shift_right(h, 16)
                        h = (h & 65535).astype(jnp.float32)
                        noise[x, l, c] = theta * (h * (1.0 / 32767.5) - 1.0)
                return carry

            lax.fori_loop(0, layers, noise_layer, 0)

        to_right.wait_recv()
        to_left.wait_recv()

        @pl.when(has_below)
        def _():
            edge_up.wait_recv()
            edge_down.wait_send()
            for c in range(3):
                masked[:, 0, c] = edge_lo[stage, :, c]

        @pl.when(has_above)
        def _():
            edge_down.wait_recv()
            edge_up.wait_send()
            for c in range(3):
                masked[:, layers + 1, c] = edge_hi[stage, :, c]

        @pl.when(jnp.logical_not(has_below))
        def _():
            for c in range(3):
                masked[:, 0, c] = nothing[c]

        @pl.when(jnp.logical_not(has_above))
        def _():
            for c in range(3):
                masked[:, layers + 1, c] = nothing[c]

        def rest_layer(l, carry):
            stiff = coefficient(stiff_ref, l)
            aniso = coefficient(aniso_ref, l)
            for c in range(3):
                lows = [halo_lo[stage, i, l, c] for i in range(2)]
                mine = [masked[x, 1 + l, c] for x in range(rows)]
                highs = [halo_hi[stage, i, l, c] for i in range(2)]
                ext = lows + mine + highs
                for x in range(rows):
                    w = mine[x]
                    prev = pltpu.roll(w, 1, axis=0)
                    after = pltpu.roll(w, SUB - 1, axis=0)
                    near = ext[x + 1] + ext[x + 3]
                    near += pltpu.roll(jnp.where(lane == LANES - 1, prev, w), 1, axis=1)
                    near += pltpu.roll(jnp.where(lane == 0, after, w), LANES - 1, axis=1)
                    far = ext[x] + ext[x + 4]
                    far += pltpu.roll(jnp.where(lane >= LANES - 2, prev, w), 2, axis=1)
                    far += pltpu.roll(jnp.where(lane < 2, after, w), LANES - 2, axis=1)
                    planar = (4.0 / 3.0) * near - (1.0 / 12.0) * far
                    vertical = masked[x, 2 + l, c] + masked[x, l, c]
                    h = stiff * (planar + 0.5 * vertical) + noise[x, l, c]
                    if c == 2:
                        h += aniso * field[x, l, c]
                    rest[x, l, c] = h
            return carry

        lax.fori_loop(0, layers, rest_layer, 0)

        @pl.when(is1)
        def _():
            across_down.wait_recv()
            outer_s = add3(read(state_in.at[stage], 1), apply(matrix(3), read(state_out, 2)))
            write(4, outer_s)
            first_s = add3(read(state_out, 1), apply(matrix(1), read(state_out, 3)))
            write(5, add3(first_s, apply(matrix(2), outer_s)))
            back_down.start()

        @pl.when(is2)
        def _():
            across_up.wait_recv()
            inflow = read(state_in.at[stage], 1)
            write(3, inflow)
            end_y = add3(read(state_out, 0), apply(matrix(0), inflow))
            write(5, end_y)
            back_up.start()
            write(4, add3(read(state_in.at[stage], 0), apply(matrix(4), end_y)))

        @pl.when(is0)
        def _():
            back_down.wait_recv()
            write(4, read(state_in.at[stage], 2))

        @pl.when(is3)
        def _():
            back_up.wait_recv()
            write(3, read(state_in.at[stage], 2))

        lax.fori_loop(0, layers, down, tuple(read(state_out, 3)))

        to_left.wait_send()
        to_right.wait_send()

        def finish_layer(k, s):
            l = layers - 1 - k
            s = apply(block_of(up_ref, first_layer + l), s)
            s = [sweep[:, l, c] - s[c] for c in range(3)]
            alpha = coefficient(damp_ref, l)
            damp = jnp.full((SUB, LANES), alpha, jnp.float32)
            scale = -1.0 / (1.0 + damp * damp)
            for x in range(rows):
                v = [field[x, l, c] for c in range(3)]
                h = [rest[x, l, c] + 0.5 * s[c][x] for c in range(3)]
                torque = cross(v, h)
                twice = cross(v, torque)
                factor = scale * maskf[x]
                change = [(torque[c] + alpha * twice[c]) * factor for c in range(3)]
                start = [base[x, l, c] for c in range(3)]
                if stage == 0:
                    moved = [start[c] + 0.03 * change[c] for c in range(3)]
                else:
                    moved = [start[c] + 0.015 * change[c] for c in range(3)]
                norm = moved[0] * moved[0] + moved[1] * moved[1] + moved[2] * moved[2]
                inverse = lax.rsqrt(norm)
                for c in range(3):
                    if stage == 0:
                        value = moved[c] * inverse
                        field[x, l, c] = value
                        masked[x, 1 + l, c] = value * maskf[x]
                        base[x, l, c] = start[c] + 0.015 * change[c]
                    else:
                        next_ref[c, l, pl.ds(x, SUB, stride=rows), :] = moved[c] * inverse
                        accum_ref[c, l, pl.ds(x, SUB, stride=rows), :] = s[c][x]
            return tuple(s)

        lax.fori_loop(0, layers, finish_layer, tuple(read(state_out, 4)))

        @pl.when(is0)
        def _():
            send_first_up.wait_send()

        @pl.when(is3)
        def _():
            send_first_down.wait_send()

        @pl.when(is1)
        def _():
            across_up.wait_send()
            back_down.wait_send()

        @pl.when(is2)
        def _():
            across_down.wait_send()
            back_up.wait_send()


def local(magnet, mask, *small):
    layers, rows, width = magnet.shape[1:]
    tiles = width // LANES

    def split(a):
        lead = a.shape[:-2]
        a = a.reshape(*lead, rows, tiles, LANES)
        return jnp.swapaxes(a, -3, -2).reshape(*lead, rows * tiles, LANES)

    def join(a):
        lead = a.shape[:-2]
        a = a.reshape(*lead, tiles, rows, LANES)
        return jnp.swapaxes(a, -3, -2).reshape(*lead, rows, width)

    small = list(small)
    for i in (6, 7, 8):
        small[i] = jnp.transpose(small[i], (1, 2, 0))
    vmem = pl.BlockSpec(memory_space=pltpu.VMEM)
    smem = pl.BlockSpec(memory_space=pltpu.SMEM)
    shape = jax.ShapeDtypeStruct((3, layers, rows * tiles, LANES), jnp.float32)
    f32 = jnp.float32
    full = (rows, layers, 3, SUB, LANES)
    state = (rows, 3, SUB, LANES)
    outs = pl.pallas_call(
        functools.partial(kernel, layers, rows),
        out_shape=(shape, shape),
        in_specs=[vmem, vmem] + [smem] * len(small),
        out_specs=(vmem, vmem),
        scratch_shapes=[
            pltpu.VMEM(full, f32),
            pltpu.VMEM(full, f32),
            pltpu.VMEM((rows, layers + 2, 3, SUB, LANES), f32),
            pltpu.VMEM(full, f32),
            pltpu.VMEM(full, f32),
            pltpu.VMEM(full, f32),
            pltpu.VMEM((rows, SUB, LANES), f32),
            pltpu.VMEM((5, 9, SUB, LANES), f32),
            pltpu.VMEM((2 * layers, 3, SUB, LANES), f32),
            pltpu.VMEM((2, 2, layers, 3, SUB, LANES), f32),
            pltpu.VMEM((2, 2, layers, 3, SUB, LANES), f32),
            pltpu.VMEM((2, *state), f32),
            pltpu.VMEM((2, *state), f32),
            pltpu.VMEM((6, *state), f32),
            pltpu.VMEM((2, 3, *state), f32),
            pltpu.SemaphoreType.DMA((16,)),
            pltpu.SemaphoreType.DMA((16,)),
        ],
        compiler_params=pltpu.CompilerParams(
            collective_id=0, has_side_effects=True, vmem_limit_bytes=32 << 20
        ),
    )(split(magnet), split(mask), *small)
    return tuple(join(a) for a in outs)


def solution(mesh):
    placed = (P(None, "depth", "plane", None), P("plane", None), P("depth")) + (P(),) * 10
    out = P(None, "depth", "plane", None)
    return jax.shard_map(
        local, mesh=mesh, in_specs=placed, out_specs=(out, out), check_vma=False
    )
```

time: 1330 us -> 58.1 us (0.04); the launches traced: 1310 us -> 57.7 us
  other arithmetic: 1070 us -> 0 us
  starting transfers between devices: 99.2 us -> 0 us
  local copies, waits for them, and re-layouts: 106 us -> 7.16 us
  Pallas kernels: 0 us -> 48.5 us
  waiting for transfers between devices: 17.6 us -> 0 us
  between operations: 16.5 us -> 2.02 us
    add x191 -> x0, other arithmetic: 1050 us -> none  [the longest x186 1040 us: apply_block(): block[row, 0] * vec[0] + block[row, 1] * vec[1] + block[row, 2] * vec[2]]
    ppermute x8 -> x0, starting transfers between devices: 55.9 us -> none  [the longest x4 28.8 us: padded(): lax.ppermute(lax.slice_in_dim(block, block.shape[dim] - width, None, axis...]
    pallas_call x0 -> x1, Pallas kernels: none -> 48.5 us  [local(): pl.pallas_call(functools.partial(kernel, layers, rows), out_shape=(shape,...]
    slice x73 -> x0, local copies, waits for them, and re-layouts: 43.4 us -> none  [the longest x49 34.9 us: apply_block(): block[row, 0] * vec[0] + block[row, 1] * vec[1] + block[row, 2] * vec[2]]
    all_to_all x4 -> x0, starting transfers between devices: 43.2 us -> none  [the longest x2 27.5 us: spin_solve(): lax.all_to_all(source, 'depth', split_axis=3, concat_axis=1, tiled=True)]
    unnamed x36 -> x24, local copies, waits for them, and re-layouts: 41 us -> 7.16 us
    all_to_all x4 -> x0, waiting for transfers between devices: 17.5 us -> none  [the longest x2 17.5 us: spin_solve(): lax.all_to_all(solved, 'depth', split_axis=1, concat_axis=3, tiled=True)]
  transfers between devices with their start and end apart: 12 -> 0, of which waited for: 1 -> 0; matrix products, arithmetic and copies ran while one was open for 87% -> 0% of each run, Pallas kernels for 0% -> 0%
where the time goes in v1:
time: 58.1 us; the launch traced here: 57.7 us
  Pallas kernels  48.5 us (83%)
  local copies, waits for them, and re-layouts  7.16 us (12%)
  between operations  2.02 us (3%)
    pallas_call x1, Pallas kernels, local(): pl.pallas_call(functools.partial(kernel, layers, rows), out_shape=(shape,...  48.5 us
    unnamed x24, local copies, waits for them, and re-layouts  7.16 us

profile of v1, /device:TPU:1, one launch (start us, length us, event | category | flops | bytes accessed | tf_op | source)
XLA Modules:
  0.0 57.7 jit_solution(2231372231858386076)
XLA Ops:
  0.6 0.0 copy-start.3
  1.3 0.0 copy-start.2
  2.0 0.0 copy-start.5
  2.0 0.0 copy-start.6
  2.0 0.0 copy-done.3
  2.0 0.0 copy-done.2
  2.0 0.6 %copy-done.5 = s32[8]{0:T(128)S(1)} copy-done((s32[8]{0:T(128)S(1)}, s32[8]{0:T(128)}, u32[]{:S(2)}) %copy-start.5) | copy-done | bytes 56
  2.6 0.0 copy-done.6
  2.6 0.0 copy-start
  2.6 1.0 %copy-done = f32[3,8,4,1024]{3,2,1,0:T(4,128)S(1)} copy-done((f32[3,8,4,1024]{3,2,1,0:T(4,128)S(1)}, f32[3,8,4,1024]{3,2,1,0:T(4,128)}, u32[]{:S(2)}) %copy-start) | copy-done | bytes 393240
  3.6 0.0 copy-start.1
  3.6 0.7 %copy-done.1 = s32[4,1024]{1,0:T(4,128)S(1)} copy-done((s32[4,1024]{1,0:T(4,128)S(1)}, s32[4,1024]{1,0:T(4,128)}, u32[]{:S(2)}) %copy-start.1) | copy-done | bytes 16408
  4.4 0.0 copy-start.4
  4.4 0.7 %copy-done.4 = f32[32,3,3]{0,2,1:T(4,128)S(1)} copy-done((f32[32,3,3]{0,2,1:T(4,128)S(1)}, f32[32,3,3]{0,2,1:T(4,128)}, u32[]{:S(2)}) %copy-start.4) | copy-done | bytes 1176
  5.1 0.0 copy-start.7
  5.1 0.7 %copy-done.7 = f32[4]{0:T(128)S(1)} copy-done((f32[4]{0:T(128)S(1)}, f32[4]{0:T(128)}, u32[]{:S(2)}) %copy-start.7) | copy-done | bytes 40
  5.7 0.0 copy-start.8
  5.7 0.7 %copy-done.8 = f32[4]{0:T(128)S(1)} copy-done((f32[4]{0:T(128)S(1)}, f32[4]{0:T(128)}, u32[]{:S(2)}) %copy-start.8) | copy-done | bytes 40
  6.4 0.0 copy-start.9
  6.4 0.7 %copy-done.9 = f32[4]{0:T(128)S(1)} copy-done((f32[4]{0:T(128)S(1)}, f32[4]{0:T(128)}, u32[]{:S(2)}) %copy-start.9) | copy-done | bytes 40
  7.0 0.0 copy-start.10
  7.0 0.7 %copy-done.10 = f32[4]{0:T(128)S(1)} copy-done((f32[4]{0:T(128)S(1)}, f32[4]{0:T(128)}, u32[]{:S(2)}) %copy-start.10) | copy-done | bytes 40
  7.7 48.5 %shard_map.140 = (f32[3,8,32,128]{3,2,1,0:T(8,128)S(1)}, f32[3,8,32,128]{3,2,1,0:T(8,128)S(1)}) custom-call(f32[3,8,32,128]{3,2,1,0:T(8,128)S(1)} %bitcast.25, s32[32,128]{1,0:T(8,128)S(1)} %bitcast.26, s32[8]{0:T(128)S(1)} %copy-done.5, f32[4]{0:T(128)S(1)} %copy-done.6, f32[4]{0:T(128)S(1)} %copy-done.7, f32[4]{0:T(128)S(1)} %copy-done.8, f32[4]{0:T(128)S(1)} %copy-done.9, ...), custom_call_target="tpu_custom_call" | custom-call | tf_op jit(solution)/shard_map/pallas_call | solution.py:462
  56.2 0.7 %copy.23 = f32[3,8,4,1024]{3,2,1,0:T(4,128)} copy(f32[3,8,4,1024]{3,2,1,0:T(4,128)S(1)} %bitcast.24) | data formatting | bytes 786432
  57.0 0.7 %copy.24 = f32[3,8,4,1024]{3,2,1,0:T(4,128)} copy(f32[3,8,4,1024]{3,2,1,0:T(4,128)S(1)} %bitcast.23) | data formatting | bytes 786432
Async XLA Ops:
  0.6 1.4 %copy-start.3 = (f32[32,3,3]{0,2,1:T(4,128)S(1)}, f32[32,3,3]{0,2,1:T(4,128)}, u32[]{:S(2)}) copy-start(f32[32,3,3]{0,2,1:T(4,128)} %param.22) | copy-start | bytes 3460
  1.3 0.7 %copy-start.2 = (f32[32,3,3]{0,2,1:T(4,128)S(1)}, f32[32,3,3]{0,2,1:T(4,128)}, u32[]{:S(2)}) copy-start(f32[32,3,3]{0,2,1:T(4,128)} %param.21) | copy-start | bytes 3460
  2.0 0.7 %copy-start.5 = (s32[8]{0:T(128)S(1)}, s32[8]{0:T(128)}, u32[]{:S(2)}) copy-start(s32[8]{0:T(128)} %mat_ref.1) | copy-start | bytes 100
  2.0 0.7 %copy-start.6 = (f32[4]{0:T(128)S(1)}, f32[4]{0:T(128)}, u32[]{:S(2)}) copy-start(f32[4]{0:T(128)} %stiff_ref.1) | copy-start | bytes 52
  2.6 1.0 %copy-start = (f32[3,8,4,1024]{3,2,1,0:T(4,128)S(1)}, f32[3,8,4,1024]{3,2,1,0:T(4,128)}, u32[]{:S(2)}) copy-start(f32[3,8,4,1024]{3,2,1,0:T(4,128)} %param.13) | copy-start | bytes 1179652
  3.6 0.7 %copy-start.1 = (s32[4,1024]{1,0:T(4,128)S(1)}, s32[4,1024]{1,0:T(4,128)}, u32[]{:S(2)}) copy-start(s32[4,1024]{1,0:T(4,128)} %param.14) | copy-start | bytes 49156
  4.4 0.7 %copy-start.4 = (f32[32,3,3]{0,2,1:T(4,128)S(1)}, f32[32,3,3]{0,2,1:T(4,128)}, u32[]{:S(2)}) copy-start(f32[32,3,3]{0,2,1:T(4,128)} %param.23) | copy-start | bytes 3460
  5.1 0.7 %copy-start.7 = (f32[4]{0:T(128)S(1)}, f32[4]{0:T(128)}, u32[]{:S(2)}) copy-start(f32[4]{0:T(128)} %aniso_ref.1) | copy-start | bytes 52
  5.7 0.7 %copy-start.8 = (f32[4]{0:T(128)S(1)}, f32[4]{0:T(128)}, u32[]{:S(2)}) copy-start(f32[4]{0:T(128)} %damp_ref.1) | copy-start | bytes 52
  6.4 0.7 %copy-start.9 = (f32[4]{0:T(128)S(1)}, f32[4]{0:T(128)}, u32[]{:S(2)}) copy-start(f32[4]{0:T(128)} %source_ref.1) | copy-start | bytes 52
  7.0 0.7 %copy-start.10 = (f32[4]{0:T(128)S(1)}, f32[4]{0:T(128)}, u32[]{:S(2)}) copy-start(f32[4]{0:T(128)} %theta_ref.1) | copy-start | bytes 52

commit v2 on v1

v2 whole, which is shorter than its diff:
```python
import functools

import jax
import jax.numpy as jnp
from jax import lax
from jax.experimental import pallas as pl
from jax.experimental.pallas import tpu as pltpu
from jax.sharding import PartitionSpec as P

MESH = pl.DeviceIdType.MESH
LANES = 128
SUB = 8
K1 = 739982445
K2 = 695872825
K3 = 1597334677


def cross(a, b):
    return [a[1] * b[2] - a[2] * b[1], a[2] * b[0] - a[0] * b[2], a[0] * b[1] - a[1] * b[0]]


def apply(block, vec):
    return [block[r][0] * vec[0] + block[r][1] * vec[1] + block[r][2] * vec[2] for r in range(3)]


def sub3(a, b):
    return [a[c] - b[c] for c in range(3)]


def add3(a, b):
    return [a[c] + b[c] for c in range(3)]


def shift_right(value, amount):
    return lax.shift_right_logical(value, jnp.full(value.shape, amount, jnp.int32))


def kernel(
    layers,
    rows,
    magnet_hbm,
    mask_hbm,
    mat_hbm,
    stiff_hbm,
    aniso_hbm,
    damp_hbm,
    source_hbm,
    theta_hbm,
    piv_hbm,
    low_hbm,
    up_hbm,
    offset_ref,
    next_ref,
    accum_ref,
    magnet_ref,
    mask_ref,
    mat_ref,
    stiff_ref,
    aniso_ref,
    damp_ref,
    source_ref,
    theta_ref,
    piv_ref,
    low_ref,
    up_ref,
    base,
    field,
    masked,
    noise,
    rest,
    sweep,
    maskf,
    coef,
    unit_y,
    halo_lo,
    halo_hi,
    edge_lo,
    edge_hi,
    state_out,
    state_in,
    relay_in,
    load_sem,
    send_sem,
    recv_sem,
    ready_sem,
):
    depth_id = lax.axis_index("depth")
    plane_id = lax.axis_index("plane")
    depth_count = lax.axis_size("depth")
    plane_count = lax.axis_size("plane")
    total_layers = layers * depth_count
    total_rows = rows * plane_count
    left = lax.rem(plane_id + plane_count - 1, plane_count)
    right = lax.rem(plane_id + 1, plane_count)
    above = depth_id + 1
    below = depth_id - 1
    has_below = depth_id > 0
    has_above = depth_id < depth_count - 1
    first_layer = depth_id * layers

    is0, is1, is2, is3 = (depth_id == k for k in range(4))
    mate = depth_id + 1 - 2 * lax.rem(depth_id, 2)
    half_run = 16 if plane_count % 32 == 0 else 1
    relay = plane_id + half_run - 2 * half_run * lax.rem(plane_id // half_run, 2)

    barrier = pltpu.get_barrier_semaphore()

    def greet(device):
        pl.semaphore_signal(barrier, inc=1, device_id=device, device_id_type=MESH)

    @pl.when(is1)
    def _():
        greet((2, plane_id))
        greet((2, relay))
        greet((1, relay))

    greet((mate, plane_id))
    greet((depth_id, left))
    greet((depth_id, right))
    expected = 3 + is1.astype(jnp.int32) + 2 * is2.astype(jnp.int32)

    small_hbm = (
        mat_hbm, stiff_hbm, aniso_hbm, damp_hbm, source_hbm, theta_hbm,
        piv_hbm, low_hbm, up_hbm,
    )
    small_refs = (
        mat_ref, stiff_ref, aniso_ref, damp_ref, source_ref, theta_ref,
        piv_ref, low_ref, up_ref,
    )
    loads = [
        pltpu.make_async_copy(magnet_hbm, magnet_ref, load_sem.at[0]),
        pltpu.make_async_copy(mask_hbm, mask_ref, load_sem.at[1]),
    ]
    for i, (src, dst) in enumerate(zip(small_hbm, small_refs)):
        loads.append(pltpu.make_async_copy(src, dst, load_sem.at[2 + i]))
    for copy in loads:
        copy.start()

    lane = lax.broadcasted_iota(jnp.int32, (SUB, LANES), 1)
    sublane = lax.broadcasted_iota(jnp.int32, (SUB, LANES), 0)

    def block_of(ref, layer):
        return [[ref[i, j, layer] for j in range(3)] for i in range(3)]

    for copy in loads:
        copy.wait()
    for x in range(rows):
        maskf[x] = mask_ref[pl.ds(x, SUB, stride=rows), :].astype(jnp.float32)

    def load_layer(l, carry):
        for c in range(3):
            for x in range(rows):
                value = magnet_ref[c, l, pl.ds(x, SUB, stride=rows), :]
                base[x, l, c] = value
                field[x, l, c] = value
                masked[0, x, 1 + l, c] = value * maskf[x]
        return carry

    lax.fori_loop(0, layers, load_layer, 0)

    def unit(offset, c):
        return (lane == offset + c).astype(jnp.float32)

    zeros = jnp.zeros((SUB, LANES), jnp.float32)

    def unit_sweep(start, count, inject, finish):
        def down(i, y):
            y = [
                jnp.where(lane // 16 == 1, jnp.where(i == inject, unit(16, c), y[c]), y[c])
                for c in range(3)
            ]
            y = apply(block_of(piv_ref, start + i), apply(block_of(low_ref, start + i), y))
            y = [-y[c] for c in range(3)]
            for c in range(3):
                unit_y[i, c] = y[c]
            return tuple(y)

        last = lax.fori_loop(0, count, down, tuple(unit(0, c) for c in range(3)))

        def up(k, s):
            i = count - 1 - k
            s = apply(block_of(up_ref, start + i), s)
            return tuple(unit_y[i, c] - s[c] for c in range(3))

        mid = lax.fori_loop(0, count - finish, up, tuple(unit(32, c) for c in range(3)))
        first = lax.fori_loop(count - finish, count, up, mid)
        return last, mid, first

    def splat(slot, vec, offset):
        for r in range(3):
            for j in range(3):
                coef[slot, r * 3 + j] = jnp.broadcast_to(
                    vec[r][:, offset + j : offset + j + 1], (SUB, LANES)
                )

    def matrix(slot):
        return [[coef[slot, r * 3 + j] for j in range(3)] for r in range(3)]

    def unit_matrices():
        last, _, first = unit_sweep(first_layer, layers, 0, 0)
        splat(0, last, 0)
        splat(1, first, 0)
        splat(2, first, 32)
        _, mid, first = unit_sweep(2 * layers, 2 * layers, layers, layers)
        splat(3, first, 0)
        splat(4, mid, 16)

    def remote(slot, src, dst, device, out_slot=None):
        return pltpu.make_async_remote_copy(
            src_ref=src,
            dst_ref=dst,
            send_sem=send_sem.at[slot if out_slot is None else out_slot],
            recv_sem=recv_sem.at[slot],
            device_id=device,
            device_id_type=MESH,
        )

    def coefficient(ref, l):
        return ref[mat_ref[l]]

    nothing = tuple(jnp.zeros((rows, SUB, LANES), jnp.float32) for _ in range(3))
    for stage in range(2):
        for c in range(3):
            masked[stage, :, 0, c] = nothing[c]
            masked[stage, :, layers + 1, c] = nothing[c]

    for stage in range(2):
        slot = 8 * stage
        to_left = remote(
            slot, masked.at[stage, 0:2, 1 : layers + 1], halo_hi.at[stage], (depth_id, left)
        )
        to_right = remote(
            slot + 1,
            masked.at[stage, rows - 2 : rows, 1 : layers + 1],
            halo_lo.at[stage],
            (depth_id, right),
        )
        top = masked.at[stage, :, layers]
        edge_up = remote(slot + 2, top, edge_lo.at[stage], (above, plane_id))
        edge_down = remote(
            slot + 3, masked.at[stage, :, 1], edge_hi.at[stage], (below, plane_id)
        )
        mine_out = state_out.at[stage]
        mine_in = state_in.at[stage]
        send_first_up = remote(slot + 4, mine_out.at[0], mine_in.at[0], (above, plane_id))
        send_first_down = remote(slot + 4, mine_out.at[1], mine_in.at[0], (below, plane_id))
        across_up = remote(slot + 5, mine_out.at[2], mine_in.at[1], (above, plane_id))
        across_down = remote(slot + 5, mine_out.at[2], mine_in.at[1], (below, plane_id))
        back_down = remote(slot + 6, mine_out.at[5], mine_in.at[2], (below, plane_id))
        back_up = remote(slot + 6, mine_out.at[5], mine_in.at[2], (above, plane_id))
        hop_edge = remote(16, top, relay_in.at[0], (1, relay))
        hop_state = remote(17, mine_out.at[2], relay_in.at[1], (1, relay))
        pass_edge = remote(2, relay_in.at[0], edge_lo.at[0], (2, relay), 18)
        pass_state = remote(5, relay_in.at[1], state_in.at[0, 1], (2, relay), 19)

        def start_edges():
            @pl.when(has_below)
            def _():
                edge_down.start()

            @pl.when(jnp.logical_or(is0, is2))
            def _():
                edge_up.start()

            @pl.when(is1)
            def _():
                if stage == 0:
                    hop_edge.start()
                else:
                    edge_up.start()

        def sources(l):
            beta = coefficient(source_ref, l)
            return [beta * field[:, l, c] for c in range(3)]

        def down(l, y):
            t = sub3(sources(l), apply(block_of(low_ref, first_layer + l), y))
            y = apply(block_of(piv_ref, first_layer + l), t)
            for c in range(3):
                sweep[:, l, c] = y[c]
            return tuple(y)

        def up(k, s):
            l = layers - 1 - k
            s = apply(block_of(up_ref, first_layer + l), s)
            return tuple(sweep[:, l, c] - s[c] for c in range(3))

        def read(ref, index):
            return [ref[index, :, c] for c in range(3)]

        def write(index, value):
            for c in range(3):
                mine_out[index, :, c] = value[c]

        if stage == 1:
            start_edges()
            to_left.start()
            to_right.start()
        end = lax.fori_loop(0, layers, down, nothing)
        write(0, end)
        if stage == 0:
            pl.semaphore_wait(barrier, expected)

            @pl.when(is2)
            def _():
                for i, other in enumerate((plane_id, relay)):
                    pl.semaphore_signal(
                        ready_sem.at[i], inc=1, device_id=(1, other), device_id_type=MESH
                    )

        @pl.when(is0)
        def _():
            send_first_up.start()

        if stage == 0:
            start_edges()
            to_left.start()
            to_right.start()
        begin = lax.fori_loop(0, layers, up, nothing)
        write(1, begin)

        @pl.when(is3)
        def _():
            send_first_down.start()

        write(3, nothing)
        write(4, nothing)
        if stage == 0:
            unit_matrices()

        @pl.when(is1)
        def _():
            send_first_up.wait_recv()
            outer = read(mine_in, 0)
            write(3, outer)
            write(2, add3(read(mine_out, 0), apply(matrix(0), outer)))
            if stage == 0:
                hop_state.start()
            else:
                across_up.start()

        @pl.when(is2)
        def _():
            send_first_down.wait_recv()
            outer = read(mine_in, 0)
            inner_s = add3(outer, apply(matrix(4), read(mine_out, 0)))
            write(2, add3(read(mine_out, 1), apply(matrix(2), inner_s)))
            across_down.start()

        if stage == 0:
            flat = (sublane * LANES + lane) * K1
            offset = offset_ref[0]

            def noise_layer(l, carry):
                theta = coefficient(theta_ref, l)
                for c in range(3):
                    for x in range(rows):
                        q = c * total_layers + first_layer + l
                        q = q * total_rows + plane_id * rows + x
                        h = flat + ((q * (SUB * LANES)) * K1 + offset)
                        h = h ^ shift_right(h, 16)
                        h = h * K1
                        h = h ^ shift_right(h, 15)
                        h = h * K2
                        h = h ^ shift_right(h, 16)
                        h = (h & 65535).astype(jnp.float32)
                        noise[x, l, c] = theta * (h * (1.0 / 32767.5) - 1.0)
                return carry

            lax.fori_loop(0, layers, noise_layer, 0)

            @pl.when(is1)
            def _():
                hop_edge.wait_recv()
                pl.semaphore_wait(ready_sem.at[1], 1)
                pass_edge.start()
                hop_state.wait_recv()
                pass_state.start()

        to_right.wait_recv()
        to_left.wait_recv()

        def rest_layer(l, carry):
            stiff = coefficient(stiff_ref, l)
            aniso = coefficient(aniso_ref, l)
            for c in range(3):
                lows = [halo_lo[stage, i, l, c] for i in range(2)]
                mine = [masked[stage, x, 1 + l, c] for x in range(rows)]
                highs = [halo_hi[stage, i, l, c] for i in range(2)]
                ext = lows + mine + highs
                for x in range(rows):
                    w = mine[x]
                    prev = pltpu.roll(w, 1, axis=0)
                    after = pltpu.roll(w, SUB - 1, axis=0)
                    near = ext[x + 1] + ext[x + 3]
                    near += pltpu.roll(jnp.where(lane == LANES - 1, prev, w), 1, axis=1)
                    near += pltpu.roll(jnp.where(lane == 0, after, w), LANES - 1, axis=1)
                    far = ext[x] + ext[x + 4]
                    far += pltpu.roll(jnp.where(lane >= LANES - 2, prev, w), 2, axis=1)
                    far += pltpu.roll(jnp.where(lane < 2, after, w), LANES - 2, axis=1)
                    planar = (4.0 / 3.0) * near - (1.0 / 12.0) * far
                    vertical = masked[stage, x, 2 + l, c] + masked[stage, x, l, c]
                    h = stiff * (planar + 0.5 * vertical) + noise[x, l, c]
                    if c == 2:
                        h += aniso * field[x, l, c]
                    rest[x, l, c] = h
            return carry

        lax.fori_loop(0, layers, rest_layer, 0)

        @pl.when(has_below)
        def _():
            edge_up.wait_recv()
            half_stiff = 0.5 * coefficient(stiff_ref, 0)
            for c in range(3):
                rest[:, 0, c] += half_stiff * edge_lo[stage, :, c]

        @pl.when(has_above)
        def _():
            edge_down.wait_recv()
            half_stiff = 0.5 * coefficient(stiff_ref, layers - 1)
            for c in range(3):
                rest[:, layers - 1, c] += half_stiff * edge_hi[stage, :, c]

        @pl.when(is1)
        def _():
            across_down.wait_recv()
            outer_s = add3(read(mine_in, 1), apply(matrix(3), read(mine_out, 2)))
            write(4, outer_s)
            first_s = add3(read(mine_out, 1), apply(matrix(1), read(mine_out, 3)))
            write(5, add3(first_s, apply(matrix(2), outer_s)))
            back_down.start()

        @pl.when(is2)
        def _():
            across_up.wait_recv()
            inflow = read(mine_in, 1)
            write(3, inflow)
            end_y = add3(read(mine_out, 0), apply(matrix(0), inflow))
            write(5, end_y)
            back_up.start()
            write(4, add3(read(mine_in, 0), apply(matrix(4), end_y)))

        @pl.when(is0)
        def _():
            back_down.wait_recv()
            write(4, read(mine_in, 2))

        @pl.when(is3)
        def _():
            back_up.wait_recv()
            write(3, read(mine_in, 2))

        lax.fori_loop(0, layers, down, tuple(read(mine_out, 3)))

        def finish_layer(k, s):
            l = layers - 1 - k
            s = apply(block_of(up_ref, first_layer + l), s)
            s = [sweep[:, l, c] - s[c] for c in range(3)]
            alpha = coefficient(damp_ref, l)
            damp = jnp.full((SUB, LANES), alpha, jnp.float32)
            scale = -1.0 / (1.0 + damp * damp)
            for x in range(rows):
                v = [field[x, l, c] for c in range(3)]
                h = [rest[x, l, c] + 0.5 * s[c][x] for c in range(3)]
                torque = cross(v, h)
                twice = cross(v, torque)
                factor = scale * maskf[x]
                change = [(torque[c] + alpha * twice[c]) * factor for c in range(3)]
                start = [base[x, l, c] for c in range(3)]
                if stage == 0:
                    moved = [start[c] + 0.03 * change[c] for c in range(3)]
                else:
                    moved = [start[c] + 0.015 * change[c] for c in range(3)]
                norm = moved[0] * moved[0] + moved[1] * moved[1] + moved[2] * moved[2]
                inverse = lax.rsqrt(norm)
                for c in range(3):
                    if stage == 0:
                        value = moved[c] * inverse
                        field[x, l, c] = value
                        masked[1, x, 1 + l, c] = value * maskf[x]
                        base[x, l, c] = start[c] + 0.015 * change[c]
                    else:
                        next_ref[c, l, pl.ds(x, SUB, stride=rows), :] = moved[c] * inverse
                        accum_ref[c, l, pl.ds(x, SUB, stride=rows), :] = s[c][x]
            return tuple(s)

        lax.fori_loop(0, layers, finish_layer, tuple(read(mine_out, 4)))
        if stage == 0:

            @pl.when(is1)
            def _():
                pl.semaphore_wait(ready_sem.at[0], 1)

        if stage == 1:
            drains.append((to_left, to_right, edge_up, edge_down))
        else:
            drains = [(to_left, to_right, edge_up, edge_down)]
        ends = [send_first_up, send_first_down, across_up, across_down, back_down, back_up]
        drains[-1] = drains[-1] + tuple(ends) + (hop_edge, hop_state, pass_edge, pass_state)

    for stage, copies in enumerate(drains):
        (to_left, to_right, edge_up, edge_down, first_up, first_down, across_up, across_down,
         back_down, back_up, hop_edge, hop_state, pass_edge, pass_state) = copies
        to_left.wait_send()
        to_right.wait_send()

        @pl.when(has_below)
        def _():
            edge_down.wait_send()

        @pl.when(jnp.logical_or(is0, is2))
        def _():
            edge_up.wait_send()

        @pl.when(is0)
        def _():
            first_up.wait_send()

        @pl.when(is3)
        def _():
            first_down.wait_send()

        @pl.when(is1)
        def _():
            back_down.wait_send()
            if stage == 0:
                for copy in (hop_edge, hop_state, pass_edge, pass_state):
                    copy.wait_send()
            else:
                edge_up.wait_send()
                across_up.wait_send()

        @pl.when(is2)
        def _():
            across_down.wait_send()
            back_up.wait_send()


def local(magnet, mask, *small):
    layers, rows, width = magnet.shape[1:]
    tiles = width // LANES

    def split(a):
        lead = a.shape[:-2]
        a = a.reshape(*lead, rows, tiles, LANES)
        return jnp.swapaxes(a, -3, -2).reshape(*lead, rows * tiles, LANES)

    def join(a):
        lead = a.shape[:-2]
        a = a.reshape(*lead, tiles, rows, LANES)
        return jnp.swapaxes(a, -3, -2).reshape(*lead, rows, width)

    small = list(small)
    for i in (6, 7, 8):
        small[i] = jnp.transpose(small[i], (1, 2, 0))
    vmem = pl.BlockSpec(memory_space=pltpu.VMEM)
    hbm = pl.BlockSpec(memory_space=pltpu.MemorySpace.HBM)
    offset = small[9] * K2 + small[10] * K3
    operands = [split(magnet), split(mask), *small[:9]]
    operands = [pltpu.with_memory_space_constraint(a, pltpu.MemorySpace.HBM) for a in operands]
    held = [pltpu.VMEM(a.shape, a.dtype) for a in operands[:2]]
    held += [pltpu.SMEM(a.shape, a.dtype) for a in operands[2:]]
    shape = jax.ShapeDtypeStruct((3, layers, rows * tiles, LANES), jnp.float32)
    f32 = jnp.float32
    full = (rows, layers, 3, SUB, LANES)
    state = (rows, 3, SUB, LANES)
    outs = pl.pallas_call(
        functools.partial(kernel, layers, rows),
        out_shape=(shape, shape),
        in_specs=[hbm] * len(operands) + [pl.BlockSpec(memory_space=pltpu.SMEM)],
        out_specs=(vmem, vmem),
        scratch_shapes=held + [
            pltpu.VMEM(full, f32),
            pltpu.VMEM(full, f32),
            pltpu.VMEM((2, rows, layers + 2, 3, SUB, LANES), f32),
            pltpu.VMEM(full, f32),
            pltpu.VMEM(full, f32),
            pltpu.VMEM(full, f32),
            pltpu.VMEM((rows, SUB, LANES), f32),
            pltpu.VMEM((5, 9, SUB, LANES), f32),
            pltpu.VMEM((2 * layers, 3, SUB, LANES), f32),
            pltpu.VMEM((2, 2, layers, 3, SUB, LANES), f32),
            pltpu.VMEM((2, 2, layers, 3, SUB, LANES), f32),
            pltpu.VMEM((2, *state), f32),
            pltpu.VMEM((2, *state), f32),
            pltpu.VMEM((2, 6, *state), f32),
            pltpu.VMEM((2, 3, *state), f32),
            pltpu.VMEM((2, *state), f32),
            pltpu.SemaphoreType.DMA((len(operands),)),
            pltpu.SemaphoreType.DMA((20,)),
            pltpu.SemaphoreType.DMA((20,)),
            pltpu.SemaphoreType.REGULAR((2,)),
        ],
        compiler_params=pltpu.CompilerParams(
            collective_id=0, has_side_effects=True, vmem_limit_bytes=32 << 20
        ),
    )(*operands, offset)
    return tuple(join(a) for a in outs)


def solution(mesh):
    placed = (P(None, "depth", "plane", None), P("plane", None), P("depth")) + (P(),) * 10
    out = P(None, "depth", "plane", None)
    return jax.shard_map(
        local, mesh=mesh, in_specs=placed, out_specs=(out, out), check_vma=False
    )
```

time: 58.1 us -> 52.2 us (0.90)
  local copies, waits for them, and re-layouts: 7.16 us -> 1.49 us
    unnamed x24 -> x2, local copies, waits for them, and re-layouts: 7.16 us -> 1.49 us
where the time goes in v2:
time: 52.2 us; the launch traced here: 52.1 us
  Pallas kernels  48.6 us (93%)
  between operations  1.94 us (4%)
  local copies, waits for them, and re-layouts  1.49 us (3%)
    pallas_call x1, Pallas kernels, local(): pl.pallas_call(functools.partial(kernel, layers, rows), out_shape=(shape,...  48.6 us
    unnamed x2, local copies, waits for them, and re-layouts  1.49 us

profile of v2, /device:TPU:1, one launch (start us, length us, event | category | flops | bytes accessed | tf_op | source)
XLA Modules:
  0.0 52.1 jit_solution(13238242670260633714)
XLA Ops:
  1.9 48.6 %shard_map.140 = (f32[3,8,32,128]{3,2,1,0:T(8,128)S(1)}, f32[3,8,32,128]{3,2,1,0:T(8,128)S(1)}) custom-call(f32[3,8,32,128]{3,2,1,0:T(8,128)} %bitcast.25, s32[32,128]{1,0:T(8,128)} %bitcast.26, s32[8]{0:T(128)} %mat_hbm.1, f32[4]{0:T(128)} %stiff_hbm.1, f32[4]{0:T(128)} %aniso_hbm.1, f32[4]{0:T(128)} %damp_hbm.1, f32[4]{0:T(128)} %source_hbm.1, ...), custom_call_target="tpu_custom_call" | custom-call | tf_op jit(solution)/shard_map/pallas_call | solution.py:568
  50.6 0.7 %copy.23 = f32[3,8,4,1024]{3,2,1,0:T(4,128)} copy(f32[3,8,4,1024]{3,2,1,0:T(4,128)S(1)} %bitcast.24) | data formatting | bytes 786432
  51.3 0.7 %copy.24 = f32[3,8,4,1024]{3,2,1,0:T(4,128)} copy(f32[3,8,4,1024]{3,2,1,0:T(4,128)S(1)} %bitcast.23) | data formatting | bytes 786432

commit v3 on v2

--- a/solution.py
+++ b/solution.py
@@ -100,8 +100,12 @@
 
     is0, is1, is2, is3 = (depth_id == k for k in range(4))
     mate = depth_id + 1 - 2 * lax.rem(depth_id, 2)
-    half_run = 16 if plane_count % 32 == 0 else 1
-    relay = plane_id + half_run - 2 * half_run * lax.rem(plane_id // half_run, 2)
+    half_run = 16 if plane_count % 32 == 0 else plane_count // 2
+    run = 2 * half_run
+    place = lax.rem(plane_id, run)
+    relay = plane_id + half_run - 2 * half_run * (place // half_run)
+    far = jnp.logical_or(place == 0, place == run - 1)
+    upper = depth_id >= 2
 
     barrier = pltpu.get_barrier_semaphore()
 
@@ -135,6 +139,20 @@
         loads.append(pltpu.make_async_copy(src, dst, load_sem.at[2 + i]))
     for copy in loads:
         copy.start()
+
+    def meet():
+        pl.semaphore_wait(barrier, expected)
+
+        @pl.when(is2)
+        def _():
+            for i, other in enumerate((plane_id, relay)):
+                pl.semaphore_signal(
+                    ready_sem.at[i], inc=1, device_id=(1, other), device_id_type=MESH
+                )
+
+    @pl.when(jnp.logical_not(far))
+    def _():
+        meet()
 
     lane = lax.broadcasted_iota(jnp.int32, (SUB, LANES), 1)
     sublane = lax.broadcasted_iota(jnp.int32, (SUB, LANES), 0)
@@ -292,30 +310,32 @@
             for c in range(3):
                 mine_out[index, :, c] = value[c]
 
-        if stage == 1:
-            start_edges()
+        def start_halos():
             to_left.start()
             to_right.start()
+
+        if stage == 1:
+
+            @pl.when(jnp.logical_not(upper))
+            def _():
+                start_halos()
+
+            start_edges()
         end = lax.fori_loop(0, layers, down, nothing)
         write(0, end)
         if stage == 0:
-            pl.semaphore_wait(barrier, expected)
-
-            @pl.when(is2)
-            def _():
-                for i, other in enumerate((plane_id, relay)):
-                    pl.semaphore_signal(
-                        ready_sem.at[i], inc=1, device_id=(1, other), device_id_type=MESH
-                    )
+
+            @pl.when(far)
+            def _():
+                meet()
 
         @pl.when(is0)
         def _():
             send_first_up.start()
 
         if stage == 0:
+            start_halos()
             start_edges()
-            to_left.start()
-            to_right.start()
         begin = lax.fori_loop(0, layers, up, nothing)
         write(1, begin)
 
@@ -377,28 +397,34 @@
                 hop_state.wait_recv()
                 pass_state.start()
 
-        to_right.wait_recv()
-        to_left.wait_recv()
+        if stage == 1:
+
+            @pl.when(upper)
+            def _():
+                start_halos()
+
+        def settle():
+            lax.fori_loop(0, layers, down, tuple(read(mine_out, 3)))
 
         def rest_layer(l, carry):
             stiff = coefficient(stiff_ref, l)
             aniso = coefficient(aniso_ref, l)
             for c in range(3):
-                lows = [halo_lo[stage, i, l, c] for i in range(2)]
                 mine = [masked[stage, x, 1 + l, c] for x in range(rows)]
-                highs = [halo_hi[stage, i, l, c] for i in range(2)]
-                ext = lows + mine + highs
                 for x in range(rows):
                     w = mine[x]
                     prev = pltpu.roll(w, 1, axis=0)
                     after = pltpu.roll(w, SUB - 1, axis=0)
-                    near = ext[x + 1] + ext[x + 3]
-                    near += pltpu.roll(jnp.where(lane == LANES - 1, prev, w), 1, axis=1)
+                    near = pltpu.roll(jnp.where(lane == LANES - 1, prev, w), 1, axis=1)
                     near += pltpu.roll(jnp.where(lane == 0, after, w), LANES - 1, axis=1)
-                    far = ext[x] + ext[x + 4]
-                    far += pltpu.roll(jnp.where(lane >= LANES - 2, prev, w), 2, axis=1)
-                    far += pltpu.roll(jnp.where(lane < 2, after, w), LANES - 2, axis=1)
-                    planar = (4.0 / 3.0) * near - (1.0 / 12.0) * far
+                    far_sum = pltpu.roll(jnp.where(lane >= LANES - 2, prev, w), 2, axis=1)
+                    far_sum += pltpu.roll(jnp.where(lane < 2, after, w), LANES - 2, axis=1)
+                    for other in range(rows):
+                        if abs(other - x) == 1:
+                            near += mine[other]
+                        elif abs(other - x) == 2:
+                            far_sum += mine[other]
+                    planar = (4.0 / 3.0) * near - (1.0 / 12.0) * far_sum
                     vertical = masked[stage, x, 2 + l, c] + masked[stage, x, l, c]
                     h = stiff * (planar + 0.5 * vertical) + noise[x, l, c]
                     if c == 2:
@@ -407,29 +433,6 @@
             return carry
 
         lax.fori_loop(0, layers, rest_layer, 0)
-
-        @pl.when(has_below)
-        def _():
-            edge_up.wait_recv()
-            half_stiff = 0.5 * coefficient(stiff_ref, 0)
-            for c in range(3):
-                rest[:, 0, c] += half_stiff * edge_lo[stage, :, c]
-
-        @pl.when(has_above)
-        def _():
-            edge_down.wait_recv()
-            half_stiff = 0.5 * coefficient(stiff_ref, layers - 1)
-            for c in range(3):
-                rest[:, layers - 1, c] += half_stiff * edge_hi[stage, :, c]
-
-        @pl.when(is1)
-        def _():
-            across_down.wait_recv()
-            outer_s = add3(read(mine_in, 1), apply(matrix(3), read(mine_out, 2)))
-            write(4, outer_s)
-            first_s = add3(read(mine_out, 1), apply(matrix(1), read(mine_out, 3)))
-            write(5, add3(first_s, apply(matrix(2), outer_s)))
-            back_down.start()
 
         @pl.when(is2)
         def _():
@@ -440,18 +443,63 @@
             write(5, end_y)
             back_up.start()
             write(4, add3(read(mine_in, 0), apply(matrix(4), end_y)))
+            settle()
+
+        @pl.when(is3)
+        def _():
+            back_up.wait_recv()
+            write(3, read(mine_in, 2))
+            settle()
+
+        @pl.when(jnp.logical_not(upper))
+        def _():
+            settle()
+
+        to_right.wait_recv()
+        to_left.wait_recv()
+
+        def halo_layer(l, carry):
+            stiff = coefficient(stiff_ref, l)
+            one = stiff * (4.0 / 3.0)
+            two = stiff * (-1.0 / 12.0)
+            for c in range(3):
+                lows = [halo_lo[stage, i, l, c] for i in range(2)]
+                highs = [halo_hi[stage, i, l, c] for i in range(2)]
+                rest[0, l, c] += one * lows[1] + two * lows[0]
+                rest[1, l, c] += two * lows[1]
+                rest[rows - 1, l, c] += one * highs[0] + two * highs[1]
+                rest[rows - 2, l, c] += two * highs[0]
+            return carry
+
+        lax.fori_loop(0, layers, halo_layer, 0)
+
+        @pl.when(has_below)
+        def _():
+            edge_up.wait_recv()
+            half_stiff = 0.5 * coefficient(stiff_ref, 0)
+            for c in range(3):
+                rest[:, 0, c] += half_stiff * edge_lo[stage, :, c]
+
+        @pl.when(has_above)
+        def _():
+            edge_down.wait_recv()
+            half_stiff = 0.5 * coefficient(stiff_ref, layers - 1)
+            for c in range(3):
+                rest[:, layers - 1, c] += half_stiff * edge_hi[stage, :, c]
+
+        @pl.when(is1)
+        def _():
+            across_down.wait_recv()
+            outer_s = add3(read(mine_in, 1), apply(matrix(3), read(mine_out, 2)))
+            write(4, outer_s)
+            first_s = add3(read(mine_out, 1), apply(matrix(1), read(mine_out, 3)))
+            write(5, add3(first_s, apply(matrix(2), outer_s)))
+            back_down.start()
 
         @pl.when(is0)
         def _():
             back_down.wait_recv()
             write(4, read(mine_in, 2))
-
-        @pl.when(is3)
-        def _():
-            back_up.wait_recv()
-            write(3, read(mine_in, 2))
-
-        lax.fori_loop(0, layers, down, tuple(read(mine_out, 3)))
 
         def finish_layer(k, s):
             l = layers - 1 - k

time: 52.2 us -> 49.8 us (0.954)
  Pallas kernels: 48.6 us -> 46.3 us
    pallas_call x1, Pallas kernels: 48.6 us -> 46.3 us  [local(): pl.pallas_call(functools.partial(kernel, layers, rows), out_shape=(shape,...]
where the time goes in v3:
time: 49.8 us; the launch traced here: 49.7 us
  Pallas kernels  46.3 us (93%)
  between operations  1.94 us (4%)
  local copies, waits for them, and re-layouts  1.49 us (3%)
    pallas_call x1, Pallas kernels, local(): pl.pallas_call(functools.partial(kernel, layers, rows), out_shape=(shape,...  46.3 us
    unnamed x2, local copies, waits for them, and re-layouts  1.49 us

profile of v3, /device:TPU:1, one launch (start us, length us, event | category | flops | bytes accessed | tf_op | source)
XLA Modules:
  0.0 49.7 jit_solution(16732226647635284361)
XLA Ops:
  1.9 46.3 %shard_map.140 = (f32[3,8,32,128]{3,2,1,0:T(8,128)S(1)}, f32[3,8,32,128]{3,2,1,0:T(8,128)S(1)}) custom-call(f32[3,8,32,128]{3,2,1,0:T(8,128)} %bitcast.25, s32[32,128]{1,0:T(8,128)} %bitcast.26, s32[8]{0:T(128)} %mat_hbm.1, f32[4]{0:T(128)} %stiff_hbm.1, f32[4]{0:T(128)} %aniso_hbm.1, f32[4]{0:T(128)} %damp_hbm.1, f32[4]{0:T(128)} %source_hbm.1, ...), custom_call_target="tpu_custom_call" | custom-call | tf_op jit(solution)/shard_map/pallas_call | solution.py:616
  48.2 0.7 %copy.23 = f32[3,8,4,1024]{3,2,1,0:T(4,128)} copy(f32[3,8,4,1024]{3,2,1,0:T(4,128)S(1)} %bitcast.24) | data formatting | bytes 786432
  48.9 0.7 %copy.24 = f32[3,8,4,1024]{3,2,1,0:T(4,128)} copy(f32[3,8,4,1024]{3,2,1,0:T(4,128)S(1)} %bitcast.23) | data formatting | bytes 786432

commit v4 on v3

--- a/solution.py
+++ b/solution.py
@@ -49,7 +49,8 @@
     piv_hbm,
     low_hbm,
     up_hbm,
-    offset_ref,
+    stream_ref,
+    count_ref,
     next_ref,
     accum_ref,
     magnet_ref,
@@ -104,7 +105,14 @@
     run = 2 * half_run
     place = lax.rem(plane_id, run)
     relay = plane_id + half_run - 2 * half_run * (place // half_run)
-    far = jnp.logical_or(place == 0, place == run - 1)
+    wrap_left = place == 0
+    wrap_right = place == run - 1
+    post_place = half_run + (1 if plane_count % 32 == 0 else 0)
+    post = jnp.logical_and(depth_id < 2, place == post_place)
+
+    def turn(shift):
+        return lax.rem(plane_id + shift + plane_count, plane_count)
+
     upper = depth_id >= 2
 
     barrier = pltpu.get_barrier_semaphore()
@@ -118,9 +126,22 @@
         greet((2, relay))
         greet((1, relay))
 
+    @pl.when(post)
+    def _():
+        for group in (depth_id, depth_id + 2):
+            greet((group, turn(-post_place)))
+            greet((group, turn(-post_place - 1)))
+
     greet((mate, plane_id))
-    greet((depth_id, left))
-    greet((depth_id, right))
+
+    @pl.when(jnp.logical_not(wrap_left))
+    def _():
+        greet((depth_id, left))
+
+    @pl.when(jnp.logical_not(wrap_right))
+    def _():
+        greet((depth_id, right))
+
     expected = 3 + is1.astype(jnp.int32) + 2 * is2.astype(jnp.int32)
 
     small_hbm = (
@@ -140,19 +161,25 @@
     for copy in loads:
         copy.start()
 
-    def meet():
-        pl.semaphore_wait(barrier, expected)
-
-        @pl.when(is2)
-        def _():
-            for i, other in enumerate((plane_id, relay)):
-                pl.semaphore_signal(
-                    ready_sem.at[i], inc=1, device_id=(1, other), device_id_type=MESH
-                )
-
-    @pl.when(jnp.logical_not(far))
+    pl.semaphore_wait(barrier, expected)
+
+    def tell(index, device):
+        pl.semaphore_signal(ready_sem.at[index], inc=1, device_id=device, device_id_type=MESH)
+
+    @pl.when(is2)
     def _():
-        meet()
+        tell(0, (1, plane_id))
+        tell(1, (1, relay))
+
+    for high in range(2):
+
+        @pl.when(jnp.logical_and(wrap_left, upper == bool(high)))
+        def _():
+            tell(2 + 2 * high, (lax.rem(depth_id, 2), turn(post_place)))
+
+        @pl.when(jnp.logical_and(wrap_right, upper == bool(high)))
+        def _():
+            tell(3 + 2 * high, (lax.rem(depth_id, 2), turn(post_place + 1)))
 
     lane = lax.broadcasted_iota(jnp.int32, (SUB, LANES), 1)
     sublane = lax.broadcasted_iota(jnp.int32, (SUB, LANES), 0)
@@ -311,8 +338,18 @@
                 mine_out[index, :, c] = value[c]
 
         def start_halos():
-            to_left.start()
-            to_right.start()
+            if stage == 1:
+                to_left.start()
+                to_right.start()
+                return
+
+            @pl.when(jnp.logical_not(wrap_left))
+            def _():
+                to_left.start()
+
+            @pl.when(jnp.logical_not(wrap_right))
+            def _():
+                to_right.start()
 
         if stage == 1:
 
@@ -323,11 +360,6 @@
             start_edges()
         end = lax.fori_loop(0, layers, down, nothing)
         write(0, end)
-        if stage == 0:
-
-            @pl.when(far)
-            def _():
-                meet()
 
         @pl.when(is0)
         def _():
@@ -336,6 +368,15 @@
         if stage == 0:
             start_halos()
             start_edges()
+
+            @pl.when(post)
+            def _():
+                for group, first in ((depth_id, 2), (depth_id + 2, 4)):
+                    pl.semaphore_wait(ready_sem.at[first], 1)
+                    pl.semaphore_wait(ready_sem.at[first + 1], 1)
+                    tell(6, (group, turn(-post_place - 1)))
+                    tell(6, (group, turn(-post_place)))
+
         begin = lax.fori_loop(0, layers, up, nothing)
         write(1, begin)
 
@@ -369,7 +410,7 @@
 
         if stage == 0:
             flat = (sublane * LANES + lane) * K1
-            offset = offset_ref[0]
+            offset = stream_ref[0] * K2 + count_ref[0] * K3
 
             def noise_layer(l, carry):
                 theta = coefficient(theta_ref, l)
@@ -388,6 +429,18 @@
                 return carry
 
             lax.fori_loop(0, layers, noise_layer, 0)
+
+            @pl.when(jnp.logical_or(wrap_left, wrap_right))
+            def _():
+                pl.semaphore_wait(ready_sem.at[6], 1)
+
+                @pl.when(wrap_left)
+                def _():
+                    to_left.start()
+
+                @pl.when(wrap_right)
+                def _():
+                    to_right.start()
 
             @pl.when(is1)
             def _():
@@ -455,6 +508,15 @@
         def _():
             settle()
 
+        @pl.when(is1)
+        def _():
+            across_down.wait_recv()
+            outer_s = add3(read(mine_in, 1), apply(matrix(3), read(mine_out, 2)))
+            write(4, outer_s)
+            first_s = add3(read(mine_out, 1), apply(matrix(1), read(mine_out, 3)))
+            write(5, add3(first_s, apply(matrix(2), outer_s)))
+            back_down.start()
+
         to_right.wait_recv()
         to_left.wait_recv()
 
@@ -486,15 +548,6 @@
             half_stiff = 0.5 * coefficient(stiff_ref, layers - 1)
             for c in range(3):
                 rest[:, layers - 1, c] += half_stiff * edge_hi[stage, :, c]
-
-        @pl.when(is1)
-        def _():
-            across_down.wait_recv()
-            outer_s = add3(read(mine_in, 1), apply(matrix(3), read(mine_out, 2)))
-            write(4, outer_s)
-            first_s = add3(read(mine_out, 1), apply(matrix(1), read(mine_out, 3)))
-            write(5, add3(first_s, apply(matrix(2), outer_s)))
-            back_down.start()
 
         @pl.when(is0)
         def _():
@@ -585,6 +638,17 @@
             back_up.wait_send()
 
 
+def place_out(next_vmem, accum_vmem, next_hbm, accum_hbm, sem):
+    copies = [
+        pltpu.make_async_copy(next_vmem, next_hbm, sem.at[0]),
+        pltpu.make_async_copy(accum_vmem, accum_hbm, sem.at[1]),
+    ]
+    for copy in copies:
+        copy.start()
+    for copy in copies:
+        copy.wait()
+
+
 def local(magnet, mask, *small):
     layers, rows, width = magnet.shape[1:]
     tiles = width // LANES
@@ -604,7 +668,6 @@
         small[i] = jnp.transpose(small[i], (1, 2, 0))
     vmem = pl.BlockSpec(memory_space=pltpu.VMEM)
     hbm = pl.BlockSpec(memory_space=pltpu.MemorySpace.HBM)
-    offset = small[9] * K2 + small[10] * K3
     operands = [split(magnet), split(mask), *small[:9]]
     operands = [pltpu.with_memory_space_constraint(a, pltpu.MemorySpace.HBM) for a in operands]
     held = [pltpu.VMEM(a.shape, a.dtype) for a in operands[:2]]
@@ -616,7 +679,7 @@
     outs = pl.pallas_call(
         functools.partial(kernel, layers, rows),
         out_shape=(shape, shape),
-        in_specs=[hbm] * len(operands) + [pl.BlockSpec(memory_space=pltpu.SMEM)],
+        in_specs=[hbm] * len(operands) + [pl.BlockSpec(memory_space=pltpu.SMEM)] * 2,
         out_specs=(vmem, vmem),
         scratch_shapes=held + [
             pltpu.VMEM(full, f32),
@@ -638,12 +701,21 @@
             pltpu.SemaphoreType.DMA((len(operands),)),
             pltpu.SemaphoreType.DMA((20,)),
             pltpu.SemaphoreType.DMA((20,)),
-            pltpu.SemaphoreType.REGULAR((2,)),
+            pltpu.SemaphoreType.REGULAR((7,)),
         ],
         compiler_params=pltpu.CompilerParams(
             collective_id=0, has_side_effects=True, vmem_limit_bytes=32 << 20
         ),
-    )(*operands, offset)
+    )(*operands, *small[9:])
+    outs = [pltpu.with_memory_space_constraint(a, pltpu.MemorySpace.VMEM) for a in outs]
+    outs = pl.pallas_call(
+        place_out,
+        out_shape=(shape, shape),
+        in_specs=[vmem, vmem],
+        out_specs=(hbm, hbm),
+        scratch_shapes=[pltpu.SemaphoreType.DMA((2,))],
+        compiler_params=pltpu.CompilerParams(has_side_effects=False),
+    )(*outs)
     return tuple(join(a) for a in outs)
 
 

time: 49.8 us -> 54 us (1.084)
  Pallas kernels: 46.3 us -> 52 us
  local copies, waits for them, and re-layouts: 1.49 us -> 0 us
    pallas_call x1, Pallas kernels: 46.3 us -> 51.1 us  [local(): pl.pallas_call(functools.partial(kernel, layers, rows), out_shape=(shape,...]
    unnamed x2 -> x0, local copies, waits for them, and re-layouts: 1.49 us -> none
    pallas_call x0 -> x1, Pallas kernels: none -> 0.89 us  [local(): pl.pallas_call(place_out, out_shape=(shape, shape), in_specs=[vmem, vmem]...]
where the time goes in v4:
time: 54 us; the launch traced here: 53.9 us
  Pallas kernels  52 us (96%)
  between operations  1.93 us (4%)
    pallas_call x1, Pallas kernels, local(): pl.pallas_call(functools.partial(kernel, layers, rows), out_shape=(shape,...  51.1 us

profile of v4, /device:TPU:1, one launch (start us, length us, event | category | flops | bytes accessed | tf_op | source)
XLA Modules:
  0.0 53.9 jit_solution(3672695474784878579)
XLA Ops:
  1.9 51.1 %shard_map.140 = (f32[3,8,32,128]{3,2,1,0:T(8,128)S(1)}, f32[3,8,32,128]{3,2,1,0:T(8,128)S(1)}) custom-call(f32[3,8,32,128]{3,2,1,0:T(8,128)} %bitcast.23, s32[32,128]{1,0:T(8,128)} %bitcast.24, s32[8]{0:T(128)} %mat_hbm.1, f32[4]{0:T(128)} %stiff_hbm.1, f32[4]{0:T(128)} %aniso_hbm.1, f32[4]{0:T(128)} %damp_hbm.1, f32[4]{0:T(128)} %source_hbm.1, ...), custom_call_target="tpu_custom_call" | custom-call | tf_op jit(solution)/shard_map/pallas_call | solution.py:679
  53.0 0.9 %shard_map.141 = (f32[3,8,32,128]{3,2,1,0:T(8,128)}, f32[3,8,32,128]{3,2,1,0:T(8,128)}) custom-call(f32[3,8,32,128]{3,2,1,0:T(8,128)S(1)} %get-tuple-element.6.next_vmem, f32[3,8,32,128]{3,2,1,0:T(8,128)S(1)} %get-tuple-element.7.accum_vmem), custom_call_target="tpu_custom_call" | custom-call | tf_op jit(solution)/shard_map/pallas_call | solution.py:711

commit v5 on v3

--- a/solution.py
+++ b/solution.py
@@ -49,7 +49,8 @@
     piv_hbm,
     low_hbm,
     up_hbm,
-    offset_ref,
+    stream_ref,
+    count_ref,
     next_ref,
     accum_ref,
     magnet_ref,
@@ -369,7 +370,7 @@
 
         if stage == 0:
             flat = (sublane * LANES + lane) * K1
-            offset = offset_ref[0]
+            offset = stream_ref[0] * K2 + count_ref[0] * K3
 
             def noise_layer(l, carry):
                 theta = coefficient(theta_ref, l)
@@ -455,6 +456,15 @@
         def _():
             settle()
 
+        @pl.when(is1)
+        def _():
+            across_down.wait_recv()
+            outer_s = add3(read(mine_in, 1), apply(matrix(3), read(mine_out, 2)))
+            write(4, outer_s)
+            first_s = add3(read(mine_out, 1), apply(matrix(1), read(mine_out, 3)))
+            write(5, add3(first_s, apply(matrix(2), outer_s)))
+            back_down.start()
+
         to_right.wait_recv()
         to_left.wait_recv()
 
@@ -486,15 +496,6 @@
             half_stiff = 0.5 * coefficient(stiff_ref, layers - 1)
             for c in range(3):
                 rest[:, layers - 1, c] += half_stiff * edge_hi[stage, :, c]
-
-        @pl.when(is1)
-        def _():
-            across_down.wait_recv()
-            outer_s = add3(read(mine_in, 1), apply(matrix(3), read(mine_out, 2)))
-            write(4, outer_s)
-            first_s = add3(read(mine_out, 1), apply(matrix(1), read(mine_out, 3)))
-            write(5, add3(first_s, apply(matrix(2), outer_s)))
-            back_down.start()
 
         @pl.when(is0)
         def _():
@@ -585,6 +586,17 @@
             back_up.wait_send()
 
 
+def place_out(next_vmem, accum_vmem, next_hbm, accum_hbm, sem):
+    copies = [
+        pltpu.make_async_copy(next_vmem, next_hbm, sem.at[0]),
+        pltpu.make_async_copy(accum_vmem, accum_hbm, sem.at[1]),
+    ]
+    for copy in copies:
+        copy.start()
+    for copy in copies:
+        copy.wait()
+
+
 def local(magnet, mask, *small):
     layers, rows, width = magnet.shape[1:]
     tiles = width // LANES
@@ -604,7 +616,6 @@
         small[i] = jnp.transpose(small[i], (1, 2, 0))
     vmem = pl.BlockSpec(memory_space=pltpu.VMEM)
     hbm = pl.BlockSpec(memory_space=pltpu.MemorySpace.HBM)
-    offset = small[9] * K2 + small[10] * K3
     operands = [split(magnet), split(mask), *small[:9]]
     operands = [pltpu.with_memory_space_constraint(a, pltpu.MemorySpace.HBM) for a in operands]
     held = [pltpu.VMEM(a.shape, a.dtype) for a in operands[:2]]
@@ -616,7 +627,7 @@
     outs = pl.pallas_call(
         functools.partial(kernel, layers, rows),
         out_shape=(shape, shape),
-        in_specs=[hbm] * len(operands) + [pl.BlockSpec(memory_space=pltpu.SMEM)],
+        in_specs=[hbm] * len(operands) + [pl.BlockSpec(memory_space=pltpu.SMEM)] * 2,
         out_specs=(vmem, vmem),
         scratch_shapes=held + [
             pltpu.VMEM(full, f32),
@@ -643,7 +654,16 @@
         compiler_params=pltpu.CompilerParams(
             collective_id=0, has_side_effects=True, vmem_limit_bytes=32 << 20
         ),
-    )(*operands, offset)
+    )(*operands, *small[9:])
+    outs = [pltpu.with_memory_space_constraint(a, pltpu.MemorySpace.VMEM) for a in outs]
+    outs = pl.pallas_call(
+        place_out,
+        out_shape=(shape, shape),
+        in_specs=[vmem, vmem],
+        out_specs=(hbm, hbm),
+        scratch_shapes=[pltpu.SemaphoreType.DMA((2,))],
+        compiler_params=pltpu.CompilerParams(has_side_effects=False),
+    )(*outs)
     return tuple(join(a) for a in outs)
 
 

time: 49.8 us -> 49.2 us (0.988)
  local copies, waits for them, and re-layouts: 1.49 us -> 0 us
  Pallas kernels: 46.3 us -> 47.1 us
    unnamed x2 -> x0, local copies, waits for them, and re-layouts: 1.49 us -> none
    pallas_call x0 -> x1, Pallas kernels: none -> 0.89 us  [local(): pl.pallas_call(place_out, out_shape=(shape, shape), in_specs=[vmem, vmem]...]
where the time goes in v5:
time: 49.2 us; the launch traced here: 49.1 us
  Pallas kernels  47.1 us (96%)
  between operations  1.93 us (4%)
    pallas_call x1, Pallas kernels, local(): pl.pallas_call(functools.partial(kernel, layers, rows), out_shape=(shape,...  46.3 us

profile of v5, /device:TPU:1, one launch (start us, length us, event | category | flops | bytes accessed | tf_op | source)
XLA Modules:
  0.0 49.1 jit_solution(17952712563502831329)
XLA Ops:
  1.9 46.3 %shard_map.140 = (f32[3,8,32,128]{3,2,1,0:T(8,128)S(1)}, f32[3,8,32,128]{3,2,1,0:T(8,128)S(1)}) custom-call(f32[3,8,32,128]{3,2,1,0:T(8,128)} %bitcast.23, s32[32,128]{1,0:T(8,128)} %bitcast.24, s32[8]{0:T(128)} %mat_hbm.1, f32[4]{0:T(128)} %stiff_hbm.1, f32[4]{0:T(128)} %aniso_hbm.1, f32[4]{0:T(128)} %damp_hbm.1, f32[4]{0:T(128)} %source_hbm.1, ...), custom_call_target="tpu_custom_call" | custom-call | tf_op jit(solution)/shard_map/pallas_call | solution.py:627
  48.2 0.9 %shard_map.141 = (f32[3,8,32,128]{3,2,1,0:T(8,128)}, f32[3,8,32,128]{3,2,1,0:T(8,128)}) custom-call(f32[3,8,32,128]{3,2,1,0:T(8,128)S(1)} %get-tuple-element.6.next_vmem, f32[3,8,32,128]{3,2,1,0:T(8,128)S(1)} %get-tuple-element.7.accum_vmem), custom_call_target="tpu_custom_call" | custom-call | tf_op jit(solution)/shard_map/pallas_call | solution.py:659

commit v6 on v5

--- a/solution.py
+++ b/solution.py
@@ -175,7 +175,7 @@
                 masked[0, x, 1 + l, c] = value * maskf[x]
         return carry
 
-    lax.fori_loop(0, layers, load_layer, 0)
+    lax.fori_loop(0, layers, load_layer, 0, unroll=2)
 
     def unit(offset, c):
         return (lane == offset + c).astype(jnp.float32)
@@ -194,14 +194,14 @@
                 unit_y[i, c] = y[c]
             return tuple(y)
 
-        last = lax.fori_loop(0, count, down, tuple(unit(0, c) for c in range(3)))
+        last = lax.fori_loop(0, count, down, tuple(unit(0, c) for c in range(3)), unroll=4)
 
         def up(k, s):
             i = count - 1 - k
             s = apply(block_of(up_ref, start + i), s)
             return tuple(unit_y[i, c] - s[c] for c in range(3))
 
-        mid = lax.fori_loop(0, count - finish, up, tuple(unit(32, c) for c in range(3)))
+        mid = lax.fori_loop(0, count - finish, up, tuple(unit(32, c) for c in range(3)), unroll=4)
         first = lax.fori_loop(count - finish, count, up, mid)
         return last, mid, first
 
@@ -322,7 +322,7 @@
                 start_halos()
 
             start_edges()
-        end = lax.fori_loop(0, layers, down, nothing)
+        end = lax.fori_loop(0, layers, down, nothing, unroll=True)
         write(0, end)
         if stage == 0:
 
@@ -337,7 +337,7 @@
         if stage == 0:
             start_halos()
             start_edges()
-        begin = lax.fori_loop(0, layers, up, nothing)
+        begin = lax.fori_loop(0, layers, up, nothing, unroll=True)
         write(1, begin)
 
         @pl.when(is3)
@@ -405,7 +405,7 @@
                 start_halos()
 
         def settle():
-            lax.fori_loop(0, layers, down, tuple(read(mine_out, 3)))
+            lax.fori_loop(0, layers, down, tuple(read(mine_out, 3)), unroll=True)
 
         def rest_layer(l, carry):
             stiff = coefficient(stiff_ref, l)
@@ -481,7 +481,7 @@
                 rest[rows - 2, l, c] += two * highs[0]
             return carry
 
-        lax.fori_loop(0, layers, halo_layer, 0)
+        lax.fori_loop(0, layers, halo_layer, 0, unroll=2)
 
         @pl.when(has_below)
         def _():
@@ -534,7 +534,7 @@
                         accum_ref[c, l, pl.ds(x, SUB, stride=rows), :] = s[c][x]
             return tuple(s)
 
-        lax.fori_loop(0, layers, finish_layer, tuple(read(mine_out, 4)))
+        lax.fori_loop(0, layers, finish_layer, tuple(read(mine_out, 4)), unroll=4)
         if stage == 0:
 
             @pl.when(is1)

time: 49.2 us -> 48.4 us (0.984)
  Pallas kernels: 47.1 us -> 46.3 us
    pallas_call x1, Pallas kernels: 46.3 us -> 45.4 us  [local(): pl.pallas_call(functools.partial(kernel, layers, rows), out_shape=(shape,...]
where the time goes in v6:
time: 48.4 us; the launch traced here: 48.3 us
  Pallas kernels  46.3 us (96%)
  between operations  1.93 us (4%)
    pallas_call x1, Pallas kernels, local(): pl.pallas_call(functools.partial(kernel, layers, rows), out_shape=(shape,...  45.4 us

profile of v6, /device:TPU:1, one launch (start us, length us, event | category | flops | bytes accessed | tf_op | source)
XLA Modules:
  0.0 48.3 jit_solution(3445056182401839034)
XLA Ops:
  1.9 45.4 %shard_map.140 = (f32[3,8,32,128]{3,2,1,0:T(8,128)S(1)}, f32[3,8,32,128]{3,2,1,0:T(8,128)S(1)}) custom-call(f32[3,8,32,128]{3,2,1,0:T(8,128)} %bitcast.23, s32[32,128]{1,0:T(8,128)} %bitcast.24, s32[8]{0:T(128)} %mat_hbm.1, f32[4]{0:T(128)} %stiff_hbm.1, f32[4]{0:T(128)} %aniso_hbm.1, f32[4]{0:T(128)} %damp_hbm.1, f32[4]{0:T(128)} %source_hbm.1, ...), custom_call_target="tpu_custom_call" | custom-call | tf_op jit(solution)/shard_map/pallas_call | solution.py:627
  47.4 0.9 %shard_map.141 = (f32[3,8,32,128]{3,2,1,0:T(8,128)}, f32[3,8,32,128]{3,2,1,0:T(8,128)}) custom-call(f32[3,8,32,128]{3,2,1,0:T(8,128)S(1)} %get-tuple-element.6.next_vmem, f32[3,8,32,128]{3,2,1,0:T(8,128)S(1)} %get-tuple-element.7.accum_vmem), custom_call_target="tpu_custom_call" | custom-call | tf_op jit(solution)/shard_map/pallas_call | solution.py:659
